TPU v7x, 128 devices: a whole 4x4x4 slice. The times are simulated.
128 devices in a mesh: req: 32 (over z, y, x_lo), exp: 4 (over x_hi, core).
Axes of the slice: x: 4 (x_hi: 2, x_lo: 2; x = x_hi * 2 + x_lo), y: 4, z: 4, core: 2. Of those that a mesh axis runs over, the one named last changes fastest.
Arguments:
- hidden_in: bfloat16 [8192, 2048], P(('req', 'exp')), may hold values from -6 to 6
- query_in: bfloat16 [8192, 2048], P('req', 'exp'), may hold values from -6 to 6
- key_in: bfloat16 [8192, 2048], P('req', 'exp'), may hold values from -6 to 6
- value_in: bfloat16 [8192, 2048], P('req', 'exp'), may hold values from -24 to 24
- query_gain: float32 [128], replicated, may hold values from 0.5 to 2.5
- key_gain: float32 [128], replicated, may hold values from 0.5 to 2.5
- cache_keys: bfloat16 [64, 32, 2048], P('req', None, 'exp'), may hold values from -400 to 400
- cache_values: bfloat16 [64, 32, 2048], P('req', None, 'exp'), may hold values from -24 to 24
- cache_block: int32 [128], replicated, may hold values from -1 to 63, as said below
- request_lengths: int32 [32, 4], P('req'), may hold values from 1 to 128, 256 in all within a row
- out_proj: bfloat16 [2048, 2048], P('exp'), may hold values from -0.125 to 0.125
- norm_gain: float32 [2048], replicated, may hold values from 0.25 to 1.75
- expert_ids: int32 [8192, 8], P(('req', 'exp')), may hold values from 0 to 63, all different within a row; in each aligned block of 64 rows (0 to 63, 64 to 127, ...) at most 10 rows name the same one
- gate_values: float32 [8192, 8], P(('req', 'exp')), may hold values from 0.4 to 1.6
- old_slots: int32 [64], replicated, may hold values from 0 to 63, each once
- new_replicas: int32 [32], replicated, may hold values from 0 to 63
- slot_weights: bfloat16 [64, 3, 2048, 1024], P('req', None, None, 'exp'), may hold values from -0.125 to 0.125
Outputs:
- layer_out: bfloat16 [8192, 2048], P(('req', 'exp'))
- replica_weights: bfloat16 [32, 3, 2048, 1024], P('req', None, None, 'exp')
Inputs may be any that keep to these rules, and one draw needn't show every extreme that they name: `cache_block`: each index of req has exactly 2 of its 4 requests with a block; every block serves exactly one request. `expert_ids`: in each aligned block of 64 rows (the rows of one device) no expert is named by more than 10 rows, a bound that some block reaches; the 8 experts of a row differ. `old_slots`: every expert is in exactly one slot. `request_lengths`: the lengths of each index of req sum to 256.
All inputs are finite; a program needn't handle non-finite values.
Results may differ from a plain program's by a relative error of at most 0.025.
Values may be sent and summed in bfloat16 or wider, within the bound.
A program may use at most 128 MiB of HBM per device.

v0:
```python
import math

import jax
import jax.numpy as jnp
from jax import lax
from jax.sharding import PartitionSpec as P


def prepare(values, gain, position):
    vector = values.astype(jnp.float32)
    scaled = vector * lax.rsqrt(jnp.mean(vector * vector, axis=-1, keepdims=True) + 1e-06) * gain
    half_size = scaled.shape[-1] // 2
    frequency = 10000.0 ** (-(jnp.arange(half_size, dtype=jnp.float32) * 2.0 / scaled.shape[-1]))
    angles = position[:, None] * frequency[None, :]
    cosine = jnp.cos(angles)[:, None, :]
    sine_part = jnp.sin(angles)[:, None, :]
    lower_half = scaled[..., :half_size]
    upper_half = scaled[..., half_size:]
    rotated = jnp.concatenate(
        [
            lower_half * cosine - upper_half * sine_part,
            upper_half * cosine + lower_half * sine_part,
        ],
        axis=-1,
    )
    return rotated.astype(jnp.bfloat16)


def compact(block_rows, slots_wanted):
    live = block_rows >= 0
    ranks = jnp.cumsum(live.astype(jnp.int32), axis=1) - 1
    request_idx = jnp.arange(block_rows.shape[1], dtype=jnp.int32)[None, :]
    chosen_blocks = []
    chosen_requests = []
    for slot_num in range(slots_wanted):
        picked = live & (ranks == slot_num)
        chosen_blocks.append(jnp.sum(jnp.where(picked, block_rows, 0), axis=1))
        chosen_requests.append(jnp.sum(jnp.where(picked, request_idx, 0), axis=1))
    return (jnp.stack(chosen_blocks, axis=1), jnp.stack(chosen_requests, axis=1))


def run_slots(inbox, slot_weights, capacity):
    sources = inbox.shape[0]
    model_width = inbox.shape[2]
    slot_count = slot_weights.shape[0]
    grouped = inbox.reshape(sources, slot_count, capacity, model_width)
    results = []
    for slot_num in range(slot_count):
        in_rows = grouped[:, slot_num].reshape(sources * capacity, model_width)
        gate_act = jnp.dot(in_rows, slot_weights[slot_num, 0], preferred_element_type=jnp.float32)
        up_act = jnp.dot(in_rows, slot_weights[slot_num, 1], preferred_element_type=jnp.float32)
        hidden = (jax.nn.silu(gate_act) * up_act).astype(jnp.bfloat16)
        partial_value = lax.dot_general(
            hidden,
            slot_weights[slot_num, 2],
            (((1,), (1,)), ((), ())),
            preferred_element_type=jnp.float32,
        )
        results.append(partial_value.reshape(sources, capacity, model_width))
    return jnp.stack(results, axis=1).reshape(sources, slot_count * capacity, model_width)


def body(
    hidden_in,
    query_in,
    key_in,
    value_in,
    query_gain,
    key_gain,
    cache_keys,
    cache_values,
    cache_block,
    request_lengths,
    out_proj,
    norm_gain,
    expert_ids,
    gate_values,
    old_slots,
    new_replicas,
    slot_weights,
):
    req_count = lax.axis_size("req")
    exp_count = lax.axis_size("exp")
    group_idx = lax.axis_index("req")
    tok_grp, width_q = query_in.shape
    tok_dev, model_width = hidden_in.shape
    head_size = query_gain.shape[0]
    head_count = width_q // head_size
    cache_dev = cache_keys.shape[0]
    pre_len = cache_keys.shape[1]
    req_grp = request_lengths.shape[1]
    lengths = request_lengths[0]
    req_ends = jnp.cumsum(lengths)
    starts = req_ends - lengths
    places = jnp.arange(tok_grp, dtype=jnp.int32)
    member = (places[:, None] >= starts[None, :]) & (places[:, None] < req_ends[None, :])
    request_idx = jnp.arange(req_grp, dtype=jnp.int32)
    segment = jnp.sum(jnp.where(member, request_idx[None, :], 0), axis=1)
    offset = places - jnp.sum(jnp.where(member, starts[None, :], 0), axis=1)
    block_rows = cache_block.reshape(req_count, req_grp)
    my_blocks = lax.dynamic_index_in_dim(block_rows, group_idx, 0, keepdims=False)
    has_cache = my_blocks >= 0
    token_cached = jnp.sum(jnp.where(member & has_cache[None, :], 1, 0), axis=1) > 0
    position = (offset + jnp.where(token_cached, pre_len, 0)).astype(jnp.float32)
    need_blocks, need_requests = compact(block_rows, cache_dev)
    my_requests = lax.dynamic_index_in_dim(need_requests, group_idx, 0, keepdims=False)
    every_keys, every_values = (
        lax.all_gather(cache_keys, "req", axis=0, tiled=True),
        lax.all_gather(cache_values, "req", axis=0, tiled=True),
    )
    wanted = lax.dynamic_index_in_dim(need_blocks, group_idx, 0, keepdims=False)
    far_keys = jnp.take(every_keys, wanted, axis=0)
    far_values = jnp.take(every_values, wanted, axis=0)
    query_n = prepare(query_in.reshape(tok_grp, head_count, head_size), query_gain, position)
    key_n = prepare(key_in.reshape(tok_grp, head_count, head_size), key_gain, position)
    keyset = jnp.concatenate(
        [key_n, far_keys.reshape(cache_dev * pre_len, head_count, head_size)], axis=0
    )
    valueset = jnp.concatenate(
        [
            value_in.reshape(tok_grp, head_count, head_size),
            far_values.reshape(cache_dev * pre_len, head_count, head_size),
        ],
        axis=0,
    )
    key_request = jnp.concatenate([segment, jnp.repeat(my_requests, pre_len)])
    allowed = segment[:, None] == key_request[None, :]
    scores = jnp.einsum("qhd,khd->hqk", query_n, keyset, preferred_element_type=jnp.float32) * (
        1.0 / math.sqrt(head_size)
    )
    scores = jnp.where(allowed[None], scores, -1e30)
    peak = jnp.max(scores, axis=-1, keepdims=True)
    expos = jnp.exp(scores - peak)
    weights = (expos / jnp.sum(expos, axis=-1, keepdims=True)).astype(jnp.bfloat16)
    attended = jnp.einsum("hqk,khd->qhd", weights, valueset, preferred_element_type=jnp.float32)
    attended = attended.astype(jnp.bfloat16).reshape(tok_grp, width_q)
    attn_out = lax.psum_scatter(
        jnp.dot(attended, out_proj, preferred_element_type=jnp.float32),
        "exp",
        scatter_dimension=0,
        tiled=True,
    )
    residual = hidden_in.astype(jnp.float32) + attn_out
    normed = (
        residual
        * lax.rsqrt(jnp.mean(residual * residual, axis=-1, keepdims=True) + 1e-06)
        * norm_gain
    ).astype(jnp.bfloat16)
    topk_count = expert_ids.shape[1]
    slot_total = old_slots.shape[0]
    slots_here = slot_weights.shape[0]
    capacity = max(2, tok_dev * topk_count * 5 // (4 * slot_total))
    slot_range = jnp.arange(slot_total, dtype=jnp.int32)
    slot_of = jnp.sum(
        jnp.where(old_slots[None, :] == slot_range[:, None], slot_range[None, :], 0), axis=1
    )
    flat_ids = expert_ids.reshape(-1)
    onehot = flat_ids[:, None] == slot_range[None, :]
    row_slot = jnp.sum(jnp.where(onehot, slot_of[None, :], 0), axis=1)
    before = jnp.cumsum(onehot.astype(jnp.int32), axis=0) - onehot.astype(jnp.int32)
    row_rank = jnp.sum(jnp.where(onehot, before, 0), axis=1)
    target = row_slot * capacity + row_rank
    send_rows = jnp.repeat(normed, topk_count, axis=0)
    outbox = jnp.zeros((slot_total * capacity, model_width), jnp.bfloat16).at[target].set(send_rows)
    outbox = outbox.reshape(req_count, slots_here * capacity, model_width)
    copies = jnp.broadcast_to(
        outbox[:, None], (req_count, exp_count, slots_here * capacity, model_width)
    )
    copies = copies.reshape(req_count * exp_count, slots_here * capacity, model_width)
    inbox = lax.all_to_all(copies, ("req", "exp"), split_axis=0, concat_axis=0, tiled=True)
    partial_value = run_slots(inbox, slot_weights, capacity).astype(jnp.bfloat16)
    returned = lax.all_to_all(
        partial_value, ("req", "exp"), split_axis=0, concat_axis=0, tiled=True
    )
    result = jnp.sum(
        returned.astype(jnp.float32).reshape(
            req_count, exp_count, slots_here * capacity, model_width
        ),
        axis=1,
    )
    result_rows = jnp.take(result.reshape(slot_total * capacity, model_width), target, axis=0)
    mixture = jnp.sum(
        result_rows.reshape(tok_dev, topk_count, model_width) * gate_values[:, :, None], axis=1
    )
    layer_out = (residual + mixture).astype(jnp.bfloat16)
    spread_slots = lax.all_to_all(slot_weights, "req", split_axis=2, concat_axis=0, tiled=True)
    replica_onehot = new_replicas[:, None] == slot_range[None, :]
    source_slot = jnp.sum(jnp.where(replica_onehot, slot_of[None, :], 0), axis=1)
    chosen_pieces = jnp.take(spread_slots, source_slot, axis=0)
    replica_weights = lax.all_to_all(chosen_pieces, "req", split_axis=0, concat_axis=2, tiled=True)
    return (layer_out, replica_weights)


def solution(mesh):
    in_specs = (
        P(("req", "exp"), None),
        P("req", "exp"),
        P("req", "exp"),
        P("req", "exp"),
        P(),
        P(),
        P("req", None, "exp"),
        P("req", None, "exp"),
        P(),
        P("req", None),
        P("exp", None),
        P(),
        P(("req", "exp"), None),
        P(("req", "exp"), None),
        P(),
        P(),
        P("req", None, None, "exp"),
    )
    out_specs = (P(("req", "exp"), None), P("req", None, None, "exp"))
    return jax.shard_map(body, mesh=mesh, in_specs=in_specs, out_specs=out_specs, check_vma=False)
```

profile of v0, /device:TPU:74, one launch (start us, length us, event | category | flops | bytes accessed | tf_op | source)
XLA Modules:
  0.0 917.7 jit_solution(13939975030181986648)
XLA Ops:
  8.7 10.5 %copy.102 = bf16[2,3,2048,256]{3,1,0,2:T(4,128)(2,1)} copy(bf16[2,3,2048,256]{3,2,1,0:T(8,128)(2,1)} %param.35) | data formatting | bytes 12582912 | tf_op args[16]
  19.2 8.7 all-to-all-start.2
  36.1 141.0 %all-gather.3.cloned.1.call-done = bf16[64,32,512]{2,1,0:T(8,128)(2,1)} async-done(((bf16[2,32,512]{2,1,0:T(8,128)(2,1)}), bf16[64,32,512]{2,1,0:T(8,128)(2,1)}) %all-gather.3.cloned.1.call-update) | async-done | bytes 2097168 | tf_op jit(solution)/shard_map/all_gather | solution.py:109
  179.2 152.2 %all-gather.5.cloned.1.call-done = bf16[64,32,512]{2,1,0:T(8,128)(2,1)} async-done(((bf16[2,32,512]{2,1,0:T(8,128)(2,1)}), bf16[64,32,512]{2,1,0:T(8,128)(2,1)}) %all-gather.5.cloned.1.call-update) | async-done | bytes 2097168 | tf_op jit(solution)/shard_map/all_gather | solution.py:108
  342.3 52.4 %reduce-scatter.2.cloned.1.call-done = f32[64,2048]{1,0:T(8,128)} async-done(((f32[256,2048]{1,0:T(8,128)}), f32[64,2048]{1,0:T(8,128)}) %reduce-scatter.2.cloned.1.call-update) | async-done | bytes 524304 | tf_op jit(solution)/shard_map/reduce_scatter | solution.py:137
  397.1 5.6 scatter_custom_fusion
  407.8 8.1 broadcast_in_dim.196
  416.0 9.2 %all-to-all-start = ((bf16[128,20,2048]{2,1,0:T(8,128)(2,1)}), bf16[128,20,2048]{2,1,0:T(8,128)(2,1)}, u32[]{:S(2)}, u32[]{:S(2)}) async-start(bf16[128,20,2048]{2,1,0:T(8,128)(2,1)} %bitcast.108), calls=%async_computation.1 | async-start | bytes 25165824 | tf_op jit(solution)/shard_map/all_to_all | solution.py:170
  433.6 5.2 gather_fusion.1
  442.7 145.0 %all-to-all-done = bf16[128,20,2048]{2,1,0:T(8,128)(2,1)} async-done(((bf16[128,20,2048]{2,1,0:T(8,128)(2,1)}), bf16[128,20,2048]{2,1,0:T(8,128)(2,1)}, u32[]{:S(2)}, u32[]{:S(2)}) %all-to-all-start) | async-done | bytes 10485792 | tf_op jit(solution)/shard_map/all_to_all | solution.py:170
  587.7 6.8 all-to-all-start.3
  594.5 12.6 %copy.93 = bf16[128,20,2048]{2,0,1:T(8,128)(2,1)} copy(bf16[128,20,2048]{2,1,0:T(8,128)(2,1)} %all-to-all-done) | data formatting | bytes 20971520 | tf_op jit(solution)/shard_map/all_to_all | solution.py:170
  607.2 10.2 %fusion.64 = (bf16[128,1,10,2048]{3,0,2,1:T(8,128)(2,1)}, bf16[128,1,10,2048]{3,0,2,1:T(8,128)(2,1)}) fusion(bf16[128,2,10,2048]{3,0,2,1:T(8,128)(2,1)} %bitcast.109), kind=kLoop, calls=%fused_computation.135 | loop fusion | bytes 20971520 | tf_op jit(solution)/shard_map/slice | solution.py:49
  617.3 9.0 copy.94
  626.4 10.0 %reshape_squeeze.6 = bf16[1280,2048]{1,0:T(8,128)(2,1)} reshape(bf16[128,1,10,2048]{3,2,0,1:T(8,128)(2,1)} %copy.94) | data formatting | bytes 10485760 | tf_op jit(solution)/shard_map/reshape;squeeze | solution.py:49
  644.1 9.0 copy.96
  653.1 10.2 %reshape_squeeze.7 = bf16[1280,2048]{1,0:T(8,128)(2,1)} reshape(bf16[128,1,10,2048]{3,2,0,1:T(8,128)(2,1)} %copy.96) | data formatting | bytes 10485760 | tf_op jit(solution)/shard_map/reshape;squeeze | solution.py:49
  681.2 9.0 pad_maximum_fusion
  690.1 14.1 %copy.98 = bf16[128,20,2048]{2,1,0:T(8,128)(2,1)} copy(bf16[128,20,2048]{2,0,1:T(8,128)(2,1)} %bitcast.110) | data formatting | bytes 20971520 | tf_op jit(solution)/shard_map/convert_element_type | solution.py:171
  704.2 10.9 %all-to-all-start.1 = ((bf16[128,20,2048]{2,1,0:T(8,128)(2,1)}), bf16[128,20,2048]{2,1,0:T(8,128)(2,1)}, u32[]{:S(2)}, u32[]{:S(2)}) async-start(bf16[128,20,2048]{2,1,0:T(8,128)(2,1)} %copy.98), calls=%async_computation.2 | async-start | bytes 25165824 | tf_op jit(solution)/shard_map/all_to_all | solution.py:172
  719.3 160.7 %all-to-all-done.1 = bf16[128,20,2048]{2,1,0:T(8,128)(2,1)} async-done(((bf16[128,20,2048]{2,1,0:T(8,128)(2,1)}), bf16[128,20,2048]{2,1,0:T(8,128)(2,1)}, u32[]{:S(2)}, u32[]{:S(2)}) %all-to-all-start.1) | async-done | bytes 10485792 | tf_op jit(solution)/shard_map/all_to_all | solution.py:172
  880.0 11.1 %convert_reduce_fusion = f32[32,20,2048]{2,1,0:T(8,128)} fusion(bf16[128,20,2048]{2,1,0:T(8,128)(2,1)} %all-to-all-done.1), kind=kLoop, calls=%fused_computation.6 | loop fusion | flops 9175040 | bytes 15728640 | tf_op jit(solution)/shard_map/reduce_sum | solution.py:175
  891.2 6.8 reshape.297
  898.0 8.1 gather_fusion
  (127 shorter events, 76.6 us)
Async XLA Ops:
  7.2 331.0 %copy-start = (bf16[512,2048]{1,0:T(8,128)(2,1)S(1)}, bf16[512,2048]{1,0:T(8,128)(2,1)}, u32[]{:S(2)}) copy-start(bf16[512,2048]{1,0:T(8,128)(2,1)} %param.29) | copy-start | bytes 6291460
  7.2 169.9 %all-gather.3.cloned.1.call-start = ((), (), s32[]{:S(2)}) async-start(), calls=%async_computation.5 | async-start | bytes 2162688 | tf_op jit(solution)/shard_map/all_gather | solution.py:109
  7.9 323.5 %all-gather.5.cloned.1.call-start = ((), (), s32[]{:S(2)}) async-start(), calls=%async_computation.6 | async-start | bytes 2162688 | tf_op jit(solution)/shard_map/all_gather | solution.py:108
  19.1 8.9 copy-start.12
  19.1 9.9 %copy-start.15 = (s32[1,4]{1,0:T(1,128)S(1)}, s32[1,4]{1,0:T(1,128)}, u32[]{:S(2)}) copy-start(s32[1,4]{1,0:T(1,128)} %param.28) | copy-start | bytes 52
  19.2 10.1 %copy-start.6 = (bf16[256,512]{1,0:T(8,128)(2,1)S(1)}, bf16[256,512]{1,0:T(8,128)(2,1)}, u32[]{:S(2)}) copy-start(bf16[256,512]{1,0:T(8,128)(2,1)} %param.20) | copy-start | bytes 786436
  19.2 10.3 %copy-start.7 = (bf16[256,512]{1,0:T(8,128)(2,1)S(1)}, bf16[256,512]{1,0:T(8,128)(2,1)}, u32[]{:S(2)}) copy-start(bf16[256,512]{1,0:T(8,128)(2,1)} %param.21) | copy-start | bytes 786436
  19.2 388.7 %all-to-all-start.2 = ((bf16[2,3,2048,256]{3,1,0,2:T(4,128)(2,1)}), bf16[2,3,2048,256]{3,1,0,2:T(4,128)(2,1)}, u32[]{:S(2)}, u32[]{:S(2)}) async-start(bf16[2,3,2048,256]{3,1,0,2:T(4,128)(2,1)} %copy.102), calls=%async_computation.3 | async-start | bytes 16777216 | tf_op jit(solution)/shard_map/all_to_all | solution.py:186
  27.9 5.6 copy-start.13
  27.9 5.6 copy-start.14
  27.9 366.8 %reduce-scatter.2.cloned.1.call-start = ((), (), s32[]{:S(2)}) async-start(), calls=%async_computation.7 | async-start | bytes 2621440 | tf_op jit(solution)/shard_map/reduce_scatter | solution.py:137
  34.9 301.6 %copy-start.8 = (bf16[256,4,128]{2,0,1:T(8,128)(2,1)S(1)}, bf16[256,4,128]{2,0,1:T(8,128)(2,1)}, u32[]{:S(2)}) copy-start(bf16[256,4,128]{2,0,1:T(8,128)(2,1)} %copy.83) | copy-start | bytes 786436
  338.2 3.9 copy-start.16
  338.2 56.6 %copy-start.5 = (bf16[64,2048]{1,0:T(8,128)(2,1)S(1)}, bf16[64,2048]{1,0:T(8,128)(2,1)}, u32[]{:S(2)}) copy-start(bf16[64,2048]{1,0:T(8,128)(2,1)} %param.19) | copy-start | bytes 786436
  338.2 57.8 %copy-start.9 = (f32[2048]{0:T(1024)S(1)}, f32[2048]{0:T(1024)}, u32[]{:S(2)}) copy-start(f32[2048]{0:T(1024)} %param.30) | copy-start | bytes 24580
  416.0 9.2 %copy-start.17 = (s32[32]{0:T(128)S(1)}, s32[32]{0:T(128)}, u32[]{:S(2)}) copy-start(s32[32]{0:T(128)} %param.34) | copy-start | bytes 388
  416.0 171.7 %all-to-all-start = ((bf16[128,20,2048]{2,1,0:T(8,128)(2,1)}), bf16[128,20,2048]{2,1,0:T(8,128)(2,1)}, u32[]{:S(2)}, u32[]{:S(2)}) async-start(bf16[128,20,2048]{2,1,0:T(8,128)(2,1)} %bitcast.108), calls=%async_computation.1 | async-start | bytes 25165824 | tf_op jit(solution)/shard_map/all_to_all | solution.py:170
  587.7 116.5 %all-to-all-start.3 = ((bf16[32,3,64,256]{3,2,1,0:T(8,128)(2,1)}), bf16[32,3,64,256]{3,2,1,0:T(8,128)(2,1)}, u32[]{:S(2)}, u32[]{:S(2)}) async-start(bf16[32,3,64,256]{3,2,1,0:T(8,128)(2,1)} %broadcast_select_fusion), calls=%async_computation.4 | async-start | bytes 6291456 | tf_op jit(solution)/shard_map/all_to_all | solution.py:190
  636.4 4.5 copy-start.2
  663.3 4.5 copy-start.3
  704.2 11.0 %copy-start.11 = (f32[64,8]{0,1:T(8,128)S(1)}, f32[64,8]{0,1:T(8,128)}, u32[]{:S(2)}) copy-start(f32[64,8]{0,1:T(8,128)} %param.32) | copy-start | bytes 6148
  704.2 175.8 %all-to-all-start.1 = ((bf16[128,20,2048]{2,1,0:T(8,128)(2,1)}), bf16[128,20,2048]{2,1,0:T(8,128)(2,1)}, u32[]{:S(2)}, u32[]{:S(2)}) async-start(bf16[128,20,2048]{2,1,0:T(8,128)(2,1)} %copy.98), calls=%async_computation.2 | async-start | bytes 25165824 | tf_op jit(solution)/shard_map/all_to_all | solution.py:172
  898.0 13.0 %copy-start.1 = (bf16[512,2048]{1,0:T(8,128)(2,1)S(1)}, bf16[512,2048]{1,0:T(8,128)(2,1)}, u32[]{:S(2)}) copy-start(bf16[512,2048]{1,0:T(8,128)(2,1)} %param.29) | copy-start | bytes 6291460
  906.1 4.1 copy-start.4
  (1 other events, 2.1 us)
Sparse Core Ops, SparseCore 0:
  9.7 167.3 all-gather.2
  178.7 152.7 all-gather.4
  340.4 54.2 reduce-scatter.1
where the time goes:
time: 928 us; the launch traced here: 918 us
  waiting for transfers between devices  653 us (70%)
  local copies, waits for them, and re-layouts  146 us (16%)
  other arithmetic  37.1 us (4%)
  starting transfers between devices  35.8 us (4%)
  matrix products  31.5 us (3%)
  between operations  14.5 us (2%)
    all_to_all x1, waiting for transfers between devices, body(): lax.all_to_all(partial_value, ('req', 'exp'), split_axis=0, concat_axis=0...  161 us
    all_gather x1, waiting for transfers between devices, body(): lax.all_gather(cache_keys, 'req', axis=0, tiled=True)  152 us
    all_to_all x1, waiting for transfers between devices, body(): lax.all_to_all(copies, ('req', 'exp'), split_axis=0, concat_axis=0, tiled...  145 us
    all_gather x1, waiting for transfers between devices, body(): lax.all_gather(cache_values, 'req', axis=0, tiled=True)  141 us
    reduce_scatter x1, waiting for transfers between devices, body(): lax.psum_scatter(jnp.dot(attended, out_proj, preferred_element_type=jnp.f...  52.4 us
    slice x3, local copies, waits for them, and re-layouts, run_slots(): in_rows = grouped[:, slot_num].reshape(sources * capacity, model_width)  28.2 us
    another operation x2, local copies, waits for them, and re-layouts, run_slots(): in_rows = grouped[:, slot_num].reshape(sources * capacity, model_width)  20.2 us
  transfers between devices with their start and end apart: 7, of which 5 were waited for; matrix products, arithmetic and copies ran while one was open for 19% of the time, Pallas kernels for 0%

commit v1 on v0

--- a/solution.py
+++ b/solution.py
@@ -104,13 +104,18 @@
     position = (offset + jnp.where(token_cached, pre_len, 0)).astype(jnp.float32)
     need_blocks, need_requests = compact(block_rows, cache_dev)
     my_requests = lax.dynamic_index_in_dim(need_requests, group_idx, 0, keepdims=False)
-    every_keys, every_values = (
-        lax.all_gather(cache_keys, "req", axis=0, tiled=True),
-        lax.all_gather(cache_values, "req", axis=0, tiled=True),
-    )
-    wanted = lax.dynamic_index_in_dim(need_blocks, group_idx, 0, keepdims=False)
-    far_keys = jnp.take(every_keys, wanted, axis=0)
-    far_values = jnp.take(every_values, wanted, axis=0)
+    key_width = cache_keys.shape[2]
+    rows_per = pre_len // req_count
+    both = jnp.concatenate([cache_keys, cache_values], axis=-1)
+    both = both.reshape(cache_dev, req_count, rows_per, 2 * key_width).transpose(1, 0, 2, 3)
+    spread = lax.all_to_all(both, "req", split_axis=0, concat_axis=0, tiled=True)
+    spread = spread.reshape(req_count * cache_dev, rows_per, 2 * key_width)
+    picked = jnp.take(spread, need_blocks.reshape(-1), axis=0)
+    picked = picked.reshape(req_count, cache_dev, rows_per, 2 * key_width)
+    gathered = lax.all_to_all(picked, "req", split_axis=0, concat_axis=0, tiled=True)
+    gathered = gathered.transpose(1, 0, 2, 3).reshape(cache_dev, pre_len, 2 * key_width)
+    far_keys = gathered[..., :key_width]
+    far_values = gathered[..., key_width:]
     query_n = prepare(query_in.reshape(tok_grp, head_count, head_size), query_gain, position)
     key_n = prepare(key_in.reshape(tok_grp, head_count, head_size), key_gain, position)
     keyset = jnp.concatenate(

time: 928 us -> 704 us (0.76)
  waiting for transfers between devices: 653 us -> 396 us
  starting transfers between devices: 35.8 us -> 64.6 us
    all_gather x2 -> x0, waiting for transfers between devices: 293 us -> none  [the longest x1 152 us: body(): lax.all_gather(cache_keys, 'req', axis=0, tiled=True)]
    all_to_all x1, waiting for transfers between devices: 0.01 us -> 37.6 us  [body(): lax.all_to_all(slot_weights, 'req', split_axis=2, concat_axis=0, tiled=True)]
    all_to_all x0 -> x2, starting transfers between devices: none -> 16.8 us  [the longest x1 8.55 us: body(): lax.all_to_all(both, 'req', split_axis=0, concat_axis=0, tiled=True)]
    all_to_all x1, starting transfers between devices: 9.2 us -> 20.8 us  [body(): lax.all_to_all(copies, ('req', 'exp'), split_axis=0, concat_axis=0, tiled...]
  transfers between devices with their start and end apart: 7 -> 7, of which waited for: 5 -> 5; matrix products, arithmetic and copies ran while one was open for 19% -> 26% of each run, Pallas kernels for 0% -> 0%
where the time goes in v1:
time: 704 us; the launch traced here: 697 us
  waiting for transfers between devices  396 us (56%)
  local copies, waits for them, and re-layouts  146 us (21%)
  starting transfers between devices  64.6 us (9%)
  other arithmetic  43.5 us (6%)
  matrix products  31.5 us (4%)
  between operations  14.8 us (2%)
    all_to_all x1, waiting for transfers between devices, body(): lax.all_to_all(partial_value, ('req', 'exp'), split_axis=0, concat_axis=0...  161 us
    all_to_all x1, waiting for transfers between devices, body(): lax.all_to_all(copies, ('req', 'exp'), split_axis=0, concat_axis=0, tiled...  145 us
    reduce_scatter x1, waiting for transfers between devices, body(): lax.psum_scatter(jnp.dot(attended, out_proj, preferred_element_type=jnp.f...  47.9 us
    all_to_all x1, waiting for transfers between devices, body(): lax.all_to_all(slot_weights, 'req', split_axis=2, concat_axis=0, tiled=True)  37.6 us
    slice x3, local copies, waits for them, and re-layouts, run_slots(): in_rows = grouped[:, slot_num].reshape(sources * capacity, model_width)  28.2 us
    all_to_all x1, starting transfers between devices, body(): lax.all_to_all(copies, ('req', 'exp'), split_axis=0, concat_axis=0, tiled...  20.8 us
    another operation x2, local copies, waits for them, and re-layouts, run_slots(): in_rows = grouped[:, slot_num].reshape(sources * capacity, model_width)  20.1 us
    unnamed x36, local copies, waits for them, and re-layouts  15.9 us
  transfers between devices with their start and end apart: 7, of which 5 were waited for; matrix products, arithmetic and copies ran while one was open for 26% of the time, Pallas kernels for 0%

profile of v1, /device:TPU:74, one launch (start us, length us, event | category | flops | bytes accessed | tf_op | source)
XLA Modules:
  0.0 696.7 jit_solution(8149768700036297165)
XLA Ops:
  9.9 8.5 %all-to-all-start = ((bf16[32,2,1,1024]{3,1,2,0:T(2,128)(2,1)}), bf16[32,2,1,1024]{3,1,2,0:T(2,128)(2,1)S(1)}, u32[]{:S(2)}, u32[]{:S(2)}) async-start(bf16[32,2,1,1024]{3,1,2,0:T(2,128)(2,1)} %maximum_bitcast_fusion), calls=%async_computation | async-start | bytes 262144 | tf_op jit(solution)/shard_map/all_to_all | solution.py:111
  33.1 10.5 %copy.125 = bf16[2,3,2048,256]{3,1,0,2:T(4,128)(2,1)} copy(bf16[2,3,2048,256]{3,2,1,0:T(8,128)(2,1)} %param.33) | data formatting | bytes 12582912 | tf_op args[16]
  45.2 8.3 %all-to-all-start.1 = ((bf16[32,2,1,1024]{3,1,2,0:T(2,128)(2,1)}), bf16[32,2,1,1024]{3,1,2,0:T(2,128)(2,1)S(1)}, u32[]{:S(2)}, u32[]{:S(2)}) async-start(bf16[32,2,1,1024]{3,1,2,0:T(2,128)(2,1)} %broadcast_select_fusion.1), calls=%async_computation.1 | async-start | bytes 262144 | tf_op jit(solution)/shard_map/all_to_all | solution.py:115
  58.6 8.6 %all-to-all-start.4 = ((bf16[2,3,2048,256]{3,1,0,2:T(4,128)(2,1)}), bf16[2,3,2048,256]{3,1,0,2:T(4,128)(2,1)}, u32[]{:S(2)}, u32[]{:S(2)}) async-start(bf16[2,3,2048,256]{3,1,0,2:T(4,128)(2,1)} %copy.125), calls=%async_computation.5 | async-start | bytes 16777216 | tf_op jit(solution)/shard_map/all_to_all | solution.py:191
  76.2 47.9 %reduce-scatter.2.cloned.1.call-done = f32[64,2048]{1,0:T(8,128)} async-done(((f32[256,2048]{1,0:T(8,128)}), f32[64,2048]{1,0:T(8,128)}) %reduce-scatter.2.cloned.1.call-update) | async-done | bytes 524304 | tf_op jit(solution)/shard_map/reduce_scatter | solution.py:142
  126.5 5.5 scatter_custom_fusion
  137.1 37.6 %all-to-all-done.4 = bf16[2,3,2048,256]{3,1,0,2:T(4,128)(2,1)} async-done(((bf16[2,3,2048,256]{3,1,0,2:T(4,128)(2,1)}), bf16[2,3,2048,256]{3,1,0,2:T(4,128)(2,1)}, u32[]{:S(2)}, u32[]{:S(2)}) %all-to-all-start.4) | async-done | bytes 6291488 | tf_op jit(solution)/shard_map/all_to_all | solution.py:191
  174.7 8.1 %broadcast_in_dim.199 = bf16[32,4,20,2048]{3,2,1,0:T(8,128)(2,1)} broadcast(bf16[32,20,2048]{2,1,0:T(8,128)(2,1)} %broadcast_in_dim.198), dimensions={0,2,3} | broadcast | bytes 13107200 | tf_op jit(solution)/shard_map/broadcast_in_dim | solution.py:171
  182.8 20.8 %all-to-all-start.2 = ((bf16[128,20,2048]{2,1,0:T(8,128)(2,1)}), bf16[128,20,2048]{2,1,0:T(8,128)(2,1)}, u32[]{:S(2)}, u32[]{:S(2)}) async-start(bf16[128,20,2048]{2,1,0:T(8,128)(2,1)} %bitcast.121), calls=%async_computation.3 | async-start | bytes 25165824 | tf_op jit(solution)/shard_map/all_to_all | solution.py:175
  221.2 144.9 %all-to-all-done.2 = bf16[128,20,2048]{2,1,0:T(8,128)(2,1)} async-done(((bf16[128,20,2048]{2,1,0:T(8,128)(2,1)}), bf16[128,20,2048]{2,1,0:T(8,128)(2,1)}, u32[]{:S(2)}, u32[]{:S(2)}) %all-to-all-start.2) | async-done | bytes 10485792 | tf_op jit(solution)/shard_map/all_to_all | solution.py:175
  366.2 7.2 %all-to-all-start.5 = ((bf16[32,3,64,256]{3,2,1,0:T(8,128)(2,1)}), bf16[32,3,64,256]{3,2,1,0:T(8,128)(2,1)}, u32[]{:S(2)}, u32[]{:S(2)}) async-start(bf16[32,3,64,256]{3,2,1,0:T(8,128)(2,1)} %broadcast_select_fusion), calls=%async_computation.6 | async-start | bytes 6291456 | tf_op jit(solution)/shard_map/all_to_all | solution.py:195
  373.4 12.7 %copy.116 = bf16[128,20,2048]{2,0,1:T(8,128)(2,1)} copy(bf16[128,20,2048]{2,1,0:T(8,128)(2,1)} %all-to-all-done.2) | data formatting | bytes 20971520 | tf_op jit(solution)/shard_map/all_to_all | solution.py:175
  386.0 10.2 %fusion.65 = (bf16[128,1,10,2048]{3,0,2,1:T(8,128)(2,1)}, bf16[128,1,10,2048]{3,0,2,1:T(8,128)(2,1)}) fusion(bf16[128,2,10,2048]{3,0,2,1:T(8,128)(2,1)} %bitcast.122), kind=kLoop, calls=%fused_computation.134 | loop fusion | bytes 20971520 | tf_op jit(solution)/shard_map/slice | solution.py:49
  396.3 9.0 %copy.117 = bf16[128,1,10,2048]{3,2,0,1:T(8,128)(2,1)} copy(bf16[128,1,10,2048]{3,0,2,1:T(8,128)(2,1)} %get-tuple-element.13) | data formatting | bytes 10485760 | tf_op jit(solution)/shard_map/slice | solution.py:49
  405.3 9.8 %reshape_squeeze.6 = bf16[1280,2048]{1,0:T(8,128)(2,1)} reshape(bf16[128,1,10,2048]{3,2,0,1:T(8,128)(2,1)} %copy.117) | data formatting | bytes 10485760 | tf_op jit(solution)/shard_map/reshape;squeeze | solution.py:49
  422.8 9.0 %copy.119 = bf16[128,1,10,2048]{3,2,0,1:T(8,128)(2,1)} copy(bf16[128,1,10,2048]{3,0,2,1:T(8,128)(2,1)} %get-tuple-element.14) | data formatting | bytes 10485760 | tf_op jit(solution)/shard_map/slice | solution.py:49
  431.8 10.2 %reshape_squeeze.7 = bf16[1280,2048]{1,0:T(8,128)(2,1)} reshape(bf16[128,1,10,2048]{3,2,0,1:T(8,128)(2,1)} %copy.119) | data formatting | bytes 10485760 | tf_op jit(solution)/shard_map/reshape;squeeze | solution.py:49
  459.9 9.0 %pad_maximum_fusion = bf16[128,2,10,2048]{3,0,2,1:T(8,128)(2,1)} fusion(bf16[128,1,10,2048]{3,0,2,1:T(8,128)(2,1)} %convert_bitcast_fusion, bf16[128,1,10,2048]{3,0,2,1:T(8,128)(2,1)} %convert_bitcast_fusion.1), kind=kLoop, calls=%fused_computation.6 | loop fusion | flops 5242880 | bytes 20971520 | tf_op jit(solution)/shard_map/stack | solution.py:60
  468.9 14.0 %copy.121 = bf16[128,20,2048]{2,1,0:T(8,128)(2,1)} copy(bf16[128,20,2048]{2,0,1:T(8,128)(2,1)} %bitcast.123) | data formatting | bytes 20971520 | tf_op jit(solution)/shard_map/convert_element_type | solution.py:176
  482.9 10.9 %all-to-all-start.3 = ((bf16[128,20,2048]{2,1,0:T(8,128)(2,1)}), bf16[128,20,2048]{2,1,0:T(8,128)(2,1)}, u32[]{:S(2)}, u32[]{:S(2)}) async-start(bf16[128,20,2048]{2,1,0:T(8,128)(2,1)} %copy.121), calls=%async_computation.4 | async-start | bytes 25165824 | tf_op jit(solution)/shard_map/all_to_all | solution.py:177
  498.0 160.7 %all-to-all-done.3 = bf16[128,20,2048]{2,1,0:T(8,128)(2,1)} async-done(((bf16[128,20,2048]{2,1,0:T(8,128)(2,1)}), bf16[128,20,2048]{2,1,0:T(8,128)(2,1)}, u32[]{:S(2)}, u32[]{:S(2)}) %all-to-all-start.3) | async-done | bytes 10485792 | tf_op jit(solution)/shard_map/all_to_all | solution.py:177
  658.8 11.1 %convert_reduce_fusion = f32[32,20,2048]{2,1,0:T(8,128)} fusion(bf16[128,20,2048]{2,1,0:T(8,128)(2,1)} %all-to-all-done.3), kind=kLoop, calls=%fused_computation.5 | loop fusion | flops 9175040 | bytes 15728640 | tf_op jit(solution)/shard_map/reduce_sum | solution.py:180
  669.9 6.8 reshape.362
  676.7 8.1 %gather_fusion.1 = f32[512,2048]{1,0:T(8,128)} fusion(f32[640,2048]{1,0:T(8,128)} %reshape.362, s32[1024]{0:T(1024)S(1)} %pad_clamp_fusion.1), kind=kCustom, calls=%fused_computation.1 | custom fusion | bytes 8390656 | tf_op jit(solution)/shard_map/jit(_take)/gather | solution.py:186
  (126 shorter events, 92.4 us)
Async XLA Ops:
  7.2 64.9 %copy-start = (bf16[512,2048]{1,0:T(8,128)(2,1)S(1)}, bf16[512,2048]{1,0:T(8,128)(2,1)}, u32[]{:S(2)}) copy-start(bf16[512,2048]{1,0:T(8,128)(2,1)} %param.27) | copy-start | bytes 6291460
  9.9 33.6 %all-to-all-start = ((bf16[32,2,1,1024]{3,1,2,0:T(2,128)(2,1)}), bf16[32,2,1,1024]{3,1,2,0:T(2,128)(2,1)S(1)}, u32[]{:S(2)}, u32[]{:S(2)}) async-start(bf16[32,2,1,1024]{3,1,2,0:T(2,128)(2,1)} %maximum_bitcast_fusion), calls=%async_computation | async-start | bytes 262144 | tf_op jit(solution)/shard_map/all_to_all | solution.py:111
  20.1 4.2 copy-start.9
  26.9 4.8 copy-start.10
  33.1 10.5 %copy-start.11 = (s32[64]{0:T(128)S(1)}, s32[64]{0:T(128)}, u32[]{:S(2)}) copy-start(s32[64]{0:T(128)} %fusion.50) | copy-start | bytes 772
  45.2 13.3 %all-to-all-start.1 = ((bf16[32,2,1,1024]{3,1,2,0:T(2,128)(2,1)}), bf16[32,2,1,1024]{3,1,2,0:T(2,128)(2,1)S(1)}, u32[]{:S(2)}, u32[]{:S(2)}) async-start(bf16[32,2,1,1024]{3,1,2,0:T(2,128)(2,1)} %broadcast_select_fusion.1), calls=%async_computation.1 | async-start | bytes 262144 | tf_op jit(solution)/shard_map/all_to_all | solution.py:115
  58.6 116.1 %all-to-all-start.4 = ((bf16[2,3,2048,256]{3,1,0,2:T(4,128)(2,1)}), bf16[2,3,2048,256]{3,1,0,2:T(4,128)(2,1)}, u32[]{:S(2)}, u32[]{:S(2)}) async-start(bf16[2,3,2048,256]{3,1,0,2:T(4,128)(2,1)} %copy.125), calls=%async_computation.5 | async-start | bytes 16777216 | tf_op jit(solution)/shard_map/all_to_all | solution.py:191
  67.2 56.9 %reduce-scatter.2.cloned.1.call-start = ((), (), s32[]{:S(2)}) async-start(), calls=%async_computation.7 | async-start | bytes 2621440 | tf_op jit(solution)/shard_map/reduce_scatter | solution.py:142
  72.0 2.1 copy-start.7
  72.0 3.9 copy-start.12
  72.0 52.1 %copy-start.5 = (bf16[64,2048]{1,0:T(8,128)(2,1)S(1)}, bf16[64,2048]{1,0:T(8,128)(2,1)}, u32[]{:S(2)}) copy-start(bf16[64,2048]{1,0:T(8,128)(2,1)} %param.17) | copy-start | bytes 786436
  72.0 53.3 %copy-start.6 = (f32[2048]{0:T(1024)S(1)}, f32[2048]{0:T(1024)}, u32[]{:S(2)}) copy-start(f32[2048]{0:T(1024)} %param.28) | copy-start | bytes 24580
  182.8 20.9 %copy-start.13 = (s32[32]{0:T(128)S(1)}, s32[32]{0:T(128)}, u32[]{:S(2)}) copy-start(s32[32]{0:T(128)} %param.32) | copy-start | bytes 388
  182.8 183.4 %all-to-all-start.2 = ((bf16[128,20,2048]{2,1,0:T(8,128)(2,1)}), bf16[128,20,2048]{2,1,0:T(8,128)(2,1)}, u32[]{:S(2)}, u32[]{:S(2)}) async-start(bf16[128,20,2048]{2,1,0:T(8,128)(2,1)} %bitcast.121), calls=%async_computation.3 | async-start | bytes 25165824 | tf_op jit(solution)/shard_map/all_to_all | solution.py:175
  366.2 116.8 %all-to-all-start.5 = ((bf16[32,3,64,256]{3,2,1,0:T(8,128)(2,1)}), bf16[32,3,64,256]{3,2,1,0:T(8,128)(2,1)}, u32[]{:S(2)}, u32[]{:S(2)}) async-start(bf16[32,3,64,256]{3,2,1,0:T(8,128)(2,1)} %broadcast_select_fusion), calls=%async_computation.6 | async-start | bytes 6291456 | tf_op jit(solution)/shard_map/all_to_all | solution.py:195
  415.1 4.5 copy-start.2
  442.0 4.5 copy-start.3
  482.9 11.0 %copy-start.8 = (f32[64,8]{0,1:T(8,128)S(1)}, f32[64,8]{0,1:T(8,128)}, u32[]{:S(2)}) copy-start(f32[64,8]{0,1:T(8,128)} %param.30) | copy-start | bytes 6148
  482.9 175.8 %all-to-all-start.3 = ((bf16[128,20,2048]{2,1,0:T(8,128)(2,1)}), bf16[128,20,2048]{2,1,0:T(8,128)(2,1)}, u32[]{:S(2)}, u32[]{:S(2)}) async-start(bf16[128,20,2048]{2,1,0:T(8,128)(2,1)} %copy.121), calls=%async_computation.4 | async-start | bytes 25165824 | tf_op jit(solution)/shard_map/all_to_all | solution.py:177
  676.7 13.0 %copy-start.1 = (bf16[512,2048]{1,0:T(8,128)(2,1)S(1)}, bf16[512,2048]{1,0:T(8,128)(2,1)}, u32[]{:S(2)}) copy-start(bf16[512,2048]{1,0:T(8,128)(2,1)} %param.27) | copy-start | bytes 6291460
  684.8 4.1 copy-start.4
Sparse Core Ops, SparseCore 0:
  74.2 49.7 reduce-scatter.1

commit v2 on v1

--- a/solution.py
+++ b/solution.py
@@ -37,27 +37,6 @@
         chosen_blocks.append(jnp.sum(jnp.where(picked, block_rows, 0), axis=1))
         chosen_requests.append(jnp.sum(jnp.where(picked, request_idx, 0), axis=1))
     return (jnp.stack(chosen_blocks, axis=1), jnp.stack(chosen_requests, axis=1))
-
-
-def run_slots(inbox, slot_weights, capacity):
-    sources = inbox.shape[0]
-    model_width = inbox.shape[2]
-    slot_count = slot_weights.shape[0]
-    grouped = inbox.reshape(sources, slot_count, capacity, model_width)
-    results = []
-    for slot_num in range(slot_count):
-        in_rows = grouped[:, slot_num].reshape(sources * capacity, model_width)
-        gate_act = jnp.dot(in_rows, slot_weights[slot_num, 0], preferred_element_type=jnp.float32)
-        up_act = jnp.dot(in_rows, slot_weights[slot_num, 1], preferred_element_type=jnp.float32)
-        hidden = (jax.nn.silu(gate_act) * up_act).astype(jnp.bfloat16)
-        partial_value = lax.dot_general(
-            hidden,
-            slot_weights[slot_num, 2],
-            (((1,), (1,)), ((), ())),
-            preferred_element_type=jnp.float32,
-        )
-        results.append(partial_value.reshape(sources, capacity, model_width))
-    return jnp.stack(results, axis=1).reshape(sources, slot_count * capacity, model_width)
 
 
 def body(
@@ -165,21 +144,39 @@
     before = jnp.cumsum(onehot.astype(jnp.int32), axis=0) - onehot.astype(jnp.int32)
     row_rank = jnp.sum(jnp.where(onehot, before, 0), axis=1)
     target = row_slot * capacity + row_rank
+    exp_idx = lax.axis_index("exp")
+    pair_bit = exp_idx % 2
+    pair_count = exp_count // 2
+    own_part = lax.dynamic_index_in_dim(slot_weights, pair_bit, 0, keepdims=False)
+    give_part = lax.dynamic_index_in_dim(slot_weights, 1 - pair_bit, 0, keepdims=False)
+    swap = [(e, e ^ 1) for e in range(exp_count)]
+    got_part = lax.ppermute(give_part, "exp", perm=swap)
     send_rows = jnp.repeat(normed, topk_count, axis=0)
     outbox = jnp.zeros((slot_total * capacity, model_width), jnp.bfloat16).at[target].set(send_rows)
-    outbox = outbox.reshape(req_count, slots_here * capacity, model_width)
+    outbox = outbox.reshape(req_count, 1, slots_here, capacity, model_width)
     copies = jnp.broadcast_to(
-        outbox[:, None], (req_count, exp_count, slots_here * capacity, model_width)
-    )
-    copies = copies.reshape(req_count * exp_count, slots_here * capacity, model_width)
+        outbox, (req_count, pair_count, slots_here, capacity, model_width)
+    )
+    copies = copies.reshape(req_count * exp_count, capacity, model_width)
     inbox = lax.all_to_all(copies, ("req", "exp"), split_axis=0, concat_axis=0, tiled=True)
-    partial_value = run_slots(inbox, slot_weights, capacity).astype(jnp.bfloat16)
+    in_rows = inbox.reshape(req_count * exp_count * capacity, model_width)
+    halves = []
+    for part in (own_part, got_part):
+        gate_act = jnp.dot(in_rows, part[0], preferred_element_type=jnp.float32)
+        up_act = jnp.dot(in_rows, part[1], preferred_element_type=jnp.float32)
+        hidden = (jax.nn.silu(gate_act) * up_act).astype(jnp.bfloat16)
+        piece = lax.dot_general(
+            hidden, part[2], (((1,), (1,)), ((), ())), preferred_element_type=jnp.float32
+        )
+        halves.append(piece.astype(jnp.bfloat16).astype(jnp.float32))
+    partial_value = (halves[0] + halves[1]).astype(jnp.bfloat16)
+    partial_value = partial_value.reshape(req_count * exp_count, capacity, model_width)
     returned = lax.all_to_all(
         partial_value, ("req", "exp"), split_axis=0, concat_axis=0, tiled=True
     )
     result = jnp.sum(
         returned.astype(jnp.float32).reshape(
-            req_count, exp_count, slots_here * capacity, model_width
+            req_count, pair_count, slots_here * capacity, model_width
         ),
         axis=1,
     )

time: 704 us -> 524 us (0.74)
  the two profiles are of different devices: /device:TPU:74 before, /device:TPU:1 now
where the time goes in v2:
time: 524 us; the launch traced here: 516 us
  waiting for transfers between devices  267 us (51%)
  local copies, waits for them, and re-layouts  104 us (20%)
  starting transfers between devices  58.9 us (11%)
  matrix products  38.3 us (7%)
  other arithmetic  32.3 us (6%)
  between operations  14.8 us (3%)
    all_to_all x1, waiting for transfers between devices, body(): lax.all_to_all(partial_value, ('req', 'exp'), split_axis=0, concat_axis=0...  93.8 us
    all_to_all x1, waiting for transfers between devices, body(): lax.all_to_all(copies, ('req', 'exp'), split_axis=0, concat_axis=0, tiled...  75.4 us
    reduce_scatter x1, waiting for transfers between devices, body(): lax.psum_scatter(jnp.dot(attended, out_proj, preferred_element_type=jnp.f...  51.5 us
    all_to_all x1, waiting for transfers between devices, body(): lax.all_to_all(slot_weights, 'req', split_axis=2, concat_axis=0, tiled=True)  38.9 us
    dot_general x2, matrix products, body(): lax.dot_general(hidden, part[2], (((1,), (1,)), ((), ())), preferred_elem...  23.5 us
    all_to_all x1, starting transfers between devices, body(): lax.all_to_all(copies, ('req', 'exp'), split_axis=0, concat_axis=0, tiled...  17.2 us
    unnamed x38, local copies, waits for them, and re-layouts  15 us
    reshape x1, local copies, waits for them, and re-layouts, body(): returned.astype(jnp.float32)  12.4 us
  transfers between devices with their start and end apart: 8, of which 5 were waited for; matrix products, arithmetic and copies ran while one was open for 24% of the time, Pallas kernels for 0%

profile of v2, /device:TPU:1, one launch (start us, length us, event | category | flops | bytes accessed | tf_op | source)
XLA Modules:
  0.0 515.5 jit_solution(947191581188605245)
XLA Ops:
  9.9 9.8 %all-to-all-start = ((bf16[32,2,1,1024]{3,1,2,0:T(2,128)(2,1)}), bf16[32,2,1,1024]{3,1,2,0:T(2,128)(2,1)S(1)}, u32[]{:S(2)}, u32[]{:S(2)}) async-start(bf16[32,2,1,1024]{3,1,2,0:T(2,128)(2,1)} %maximum_bitcast_fusion), calls=%async_computation | async-start | bytes 262144 | tf_op jit(solution)/shard_map/all_to_all | solution.py:90
  32.8 10.5 %copy.97 = bf16[2,3,2048,256]{3,1,0,2:T(4,128)(2,1)} copy(bf16[2,3,2048,256]{3,2,1,0:T(8,128)(2,1)} %param.33) | data formatting | bytes 12582912 | tf_op args[16]
  45.0 7.7 %all-to-all-start.1 = ((bf16[32,2,1,1024]{3,1,2,0:T(2,128)(2,1)}), bf16[32,2,1,1024]{3,1,2,0:T(2,128)(2,1)S(1)}, u32[]{:S(2)}, u32[]{:S(2)}) async-start(bf16[32,2,1,1024]{3,1,2,0:T(2,128)(2,1)} %broadcast_select_fusion.1), calls=%async_computation.1 | async-start | bytes 262144 | tf_op jit(solution)/shard_map/all_to_all | solution.py:94
  52.8 7.4 %all-to-all-done.1 = bf16[32,2,1,1024]{3,1,2,0:T(2,128)(2,1)S(1)} async-done(((bf16[32,2,1,1024]{3,1,2,0:T(2,128)(2,1)}), bf16[32,2,1,1024]{3,1,2,0:T(2,128)(2,1)S(1)}, u32[]{:S(2)}, u32[]{:S(2)}) %all-to-all-start.1) | async-done | bytes 131104 | tf_op jit(solution)/shard_map/all_to_all | solution.py:94
  74.6 51.5 %reduce-scatter.2.cloned.1.call-done = f32[64,2048]{1,0:T(8,128)} async-done(((f32[256,2048]{1,0:T(8,128)}), f32[64,2048]{1,0:T(8,128)}) %reduce-scatter.2.cloned.1.call-update) | async-done | bytes 524304 | tf_op jit(solution)/shard_map/reduce_scatter | solution.py:121
  128.5 5.4 %scatter_custom_fusion = bf16[640,2048]{1,0:T(8,128)(2,1)} fusion(s32[512]{0:T(512)S(1)} %bitcast.121, bf16[]{:T(256)} %constant.127.clone.1, bf16[64,2048]{1,0:T(8,128)(2,1)S(1)} %multiply_convert_fusion.1), kind=kCustom, calls=%fused_computation.15 | custom fusion | bytes 2883586 | tf_op jit(solution)/shard_map/scatter | solution.py:155
  133.9 5.4 %broadcast_in_dim.198 = bf16[32,2,10,2048]{3,2,1,0:T(8,128)(2,1)} reshape(bf16[640,2048]{1,0:T(8,128)(2,1)} %scatter_custom_fusion) | data formatting | bytes 5242880 | tf_op jit(solution)/shard_map/broadcast_in_dim | solution.py:157
  139.2 38.9 %all-to-all-done.4 = bf16[2,3,2048,256]{3,1,0,2:T(4,128)(2,1)} async-done(((bf16[2,3,2048,256]{3,1,0,2:T(4,128)(2,1)}), bf16[2,3,2048,256]{3,1,0,2:T(4,128)(2,1)}, u32[]{:S(2)}, u32[]{:S(2)}) %all-to-all-start.4) | async-done | bytes 6291488 | tf_op jit(solution)/shard_map/all_to_all | solution.py:188
  178.1 6.7 %broadcast_in_dim.199 = bf16[32,2,2,10,2048]{4,3,2,1,0:T(8,128)(2,1)} broadcast(bf16[32,2,10,2048]{3,2,1,0:T(8,128)(2,1)} %broadcast_in_dim.198), dimensions={0,2,3,4} | broadcast | bytes 7864320 | tf_op jit(solution)/shard_map/broadcast_in_dim | solution.py:157
  184.9 17.2 %all-to-all-start.2 = ((bf16[128,10,2048]{2,1,0:T(8,128)(2,1)}), bf16[128,10,2048]{2,1,0:T(8,128)(2,1)}, u32[]{:S(2)}, u32[]{:S(2)}) async-start(bf16[128,10,2048]{2,1,0:T(8,128)(2,1)} %bitcast.111), calls=%async_computation.3 | async-start | bytes 16777216 | tf_op jit(solution)/shard_map/all_to_all | solution.py:161
  215.5 5.3 %gather_fusion.2 = bf16[32,3,64,256]{3,2,1,0:T(8,128)(2,1)} fusion(bf16[64,3,64,256]{3,2,1,0:T(8,128)(2,1)} %bitcast.113, s32[1024]{0:T(1024)S(1)} %pad_clamp_fusion), kind=kCustom, calls=%fused_computation.2 | custom fusion | bytes 6291584 | tf_op jit(solution)/shard_map/jit(_take)/gather | solution.py:191
  224.8 75.4 %all-to-all-done.2 = bf16[128,10,2048]{2,1,0:T(8,128)(2,1)} async-done(((bf16[128,10,2048]{2,1,0:T(8,128)(2,1)}), bf16[128,10,2048]{2,1,0:T(8,128)(2,1)}, u32[]{:S(2)}, u32[]{:S(2)}) %all-to-all-start.2) | async-done | bytes 5242912 | tf_op jit(solution)/shard_map/all_to_all | solution.py:161
  300.1 7.8 %all-to-all-start.5 = ((bf16[32,3,64,256]{3,2,1,0:T(8,128)(2,1)}), bf16[32,3,64,256]{3,2,1,0:T(8,128)(2,1)}, u32[]{:S(2)}, u32[]{:S(2)}) async-start(bf16[32,3,64,256]{3,2,1,0:T(8,128)(2,1)} %broadcast_select_fusion), calls=%async_computation.6 | async-start | bytes 6291456 | tf_op jit(solution)/shard_map/all_to_all | solution.py:192
  308.0 9.9 %reshape.351 = bf16[1280,2048]{1,0:T(8,128)(2,1)} reshape(bf16[128,10,2048]{2,1,0:T(8,128)(2,1)} %all-to-all-done.2) | data formatting | bytes 10485760 | tf_op jit(solution)/shard_map/reshape | solution.py:162
  317.8 5.5 %fusion.12 = f32[1280,256]{1,0:T(8,128)} fusion(bf16[1280,2048]{1,0:T(8,128)(2,1)} %reshape.351, bf16[2,3,2048,256]{3,2,1,0:T(8,128)(2,1)} %param.33, s32[]{:T(128)S(6)} %select_n.165), kind=kOutput, calls=%fused_computation.33 | convolution fusion | flops 1342177280 | bytes 7602180 | tf_op jit(solution)/shard_map/dot_general | solution.py:165
  326.2 11.1 %convolution_convert_fusion.1 = bf16[1280,2048]{1,0:T(8,128)(2,1)} fusion(bf16[1280,2048]{1,0:T(8,128)(2,1)} %reshape.351, f32[1280,256]{1,0:T(8,128)} %fusion.12, bf16[2,3,2048,256]{3,2,1,0:T(8,128)(2,1)} %param.33, s32[]{:T(128)S(6)} %select_n.165, s32[]{:T(128)S(6)} %add.200, s32[]{:T(128)S(6)} %add.199), kind=kOutput, calls=%fused_computation.7 | convolution fusion | flops 2688942080 | bytes 13895680 | tf_op jit(solution)/shard_map/dot_general | solution.py:168
  337.3 12.4 %add_convert_fusion = bf16[1280,2048]{1,0:T(8,128)(2,1)} fusion(bf16[1280,2048]{1,0:T(8,128)(2,1)} %convolution_convert_fusion.1, bf16[3,2048,256]{2,1,0:T(8,128)(2,1)} %collective-permute-done, f32[1280,256]{1,0:T(8,128)S(1)} %fusion.11, bf16[1280,2048]{1,0:T(8,128)(2,1)} %reshape.351), kind=kOutput, calls=%fused_computation.5 | convolution fusion | flops 2699427840 | bytes 19136512 | tf_op jit(solution)/shard_map/dot_general | solution.py:168
  349.7 9.5 %reshape.352 = bf16[128,10,2048]{2,1,0:T(8,128)(2,1)} reshape(bf16[1280,2048]{1,0:T(8,128)(2,1)} %add_convert_fusion) | data formatting | bytes 10485760 | tf_op jit(solution)/shard_map/reshape | solution.py:173
  359.2 9.7 %all-to-all-start.3 = ((bf16[128,10,2048]{2,1,0:T(8,128)(2,1)}), bf16[128,10,2048]{2,1,0:T(8,128)(2,1)}, u32[]{:S(2)}, u32[]{:S(2)}) async-start(bf16[128,10,2048]{2,1,0:T(8,128)(2,1)} %reshape.352), calls=%async_computation.4 | async-start | bytes 16777216 | tf_op jit(solution)/shard_map/all_to_all | solution.py:174
  373.1 93.8 %all-to-all-done.3 = bf16[128,10,2048]{2,1,0:T(8,128)(2,1)} async-done(((bf16[128,10,2048]{2,1,0:T(8,128)(2,1)}), bf16[128,10,2048]{2,1,0:T(8,128)(2,1)}, u32[]{:S(2)}, u32[]{:S(2)}) %all-to-all-start.3) | async-done | bytes 5242912 | tf_op jit(solution)/shard_map/all_to_all | solution.py:174
  466.9 12.4 %reshape.359 = f32[32,2,20,2048]{3,2,1,0:T(8,128)} reshape(bf16[128,10,2048]{2,1,0:T(8,128)(2,1)} %all-to-all-done.3) | data formatting | bytes 15728640 | tf_op jit(solution)/shard_map/reshape | solution.py:178
  479.3 9.4 %reduce_sum.169 = f32[32,20,2048]{2,1,0:T(8,128)} reduce(f32[32,2,20,2048]{3,2,1,0:T(8,128)} %reshape.359, f32[]{:T(128)} %constant.116.clone.1), dimensions={1}, to_apply=%region_21.22 | reduce | flops 1310720 | bytes 15728644 | tf_op jit(solution)/shard_map/reduce_sum | solution.py:177
  488.7 6.8 %reshape.355 = f32[640,2048]{1,0:T(8,128)} reshape(f32[32,20,2048]{2,1,0:T(8,128)} %reduce_sum.169) | data formatting | bytes 10485760 | tf_op jit(solution)/shard_map/reshape | solution.py:183
  495.5 8.1 %gather_fusion.1 = f32[512,2048]{1,0:T(8,128)} fusion(f32[640,2048]{1,0:T(8,128)} %reshape.355, s32[1024]{0:T(1024)S(1)} %pad_clamp_fusion.1), kind=kCustom, calls=%fused_computation.1 | custom fusion | bytes 8390656 | tf_op jit(solution)/shard_map/jit(_take)/gather | solution.py:183
  (121 shorter events, 63.1 us)
Async XLA Ops:
  7.2 63.2 %copy-start = (bf16[512,2048]{1,0:T(8,128)(2,1)S(1)}, bf16[512,2048]{1,0:T(8,128)(2,1)}, u32[]{:S(2)}) copy-start(bf16[512,2048]{1,0:T(8,128)(2,1)} %param.27) | copy-start | bytes 6291460
  9.9 33.4 %all-to-all-start = ((bf16[32,2,1,1024]{3,1,2,0:T(2,128)(2,1)}), bf16[32,2,1,1024]{3,1,2,0:T(2,128)(2,1)S(1)}, u32[]{:S(2)}, u32[]{:S(2)}) async-start(bf16[32,2,1,1024]{3,1,2,0:T(2,128)(2,1)} %maximum_bitcast_fusion), calls=%async_computation | async-start | bytes 262144 | tf_op jit(solution)/shard_map/all_to_all | solution.py:90
  21.4 3.1 copy-start.9
  23.1 1.4 copy-start.12
  27.6 4.8 copy-start.10
  31.2 1.3 copy-start.5
  32.8 10.5 %copy-start.11 = (s32[64]{0:T(128)S(1)}, s32[64]{0:T(128)}, u32[]{:S(2)}) copy-start(s32[64]{0:T(128)} %fusion.42) | copy-start | bytes 772
  45.0 15.3 %all-to-all-start.1 = ((bf16[32,2,1,1024]{3,1,2,0:T(2,128)(2,1)}), bf16[32,2,1,1024]{3,1,2,0:T(2,128)(2,1)S(1)}, u32[]{:S(2)}, u32[]{:S(2)}) async-start(bf16[32,2,1,1024]{3,1,2,0:T(2,128)(2,1)} %broadcast_select_fusion.1), calls=%async_computation.1 | async-start | bytes 262144 | tf_op jit(solution)/shard_map/all_to_all | solution.py:94
  60.3 117.8 %all-to-all-start.4 = ((bf16[2,3,2048,256]{3,1,0,2:T(4,128)(2,1)}), bf16[2,3,2048,256]{3,1,0,2:T(4,128)(2,1)}, u32[]{:S(2)}, u32[]{:S(2)}) async-start(bf16[2,3,2048,256]{3,1,0,2:T(4,128)(2,1)} %copy.97), calls=%async_computation.5 | async-start | bytes 16777216 | tf_op jit(solution)/shard_map/all_to_all | solution.py:188
  65.3 60.8 %reduce-scatter.2.cloned.1.call-start = ((), (), s32[]{:S(2)}) async-start(), calls=%async_computation.7 | async-start | bytes 2621440 | tf_op jit(solution)/shard_map/reduce_scatter | solution.py:121
  70.4 2.1 copy-start.7
  70.4 3.9 copy-start.13
  70.4 55.7 %copy-start.4 = (bf16[64,2048]{1,0:T(8,128)(2,1)S(1)}, bf16[64,2048]{1,0:T(8,128)(2,1)}, u32[]{:S(2)}) copy-start(bf16[64,2048]{1,0:T(8,128)(2,1)} %param.17) | copy-start | bytes 786436
  70.4 56.9 %copy-start.6 = (f32[2048]{0:T(1024)S(1)}, f32[2048]{0:T(1024)}, u32[]{:S(2)}) copy-start(f32[2048]{0:T(1024)} %param.28) | copy-start | bytes 24580
  184.9 115.2 %all-to-all-start.2 = ((bf16[128,10,2048]{2,1,0:T(8,128)(2,1)}), bf16[128,10,2048]{2,1,0:T(8,128)(2,1)}, u32[]{:S(2)}, u32[]{:S(2)}) async-start(bf16[128,10,2048]{2,1,0:T(8,128)(2,1)} %bitcast.111), calls=%async_computation.3 | async-start | bytes 16777216 | tf_op jit(solution)/shard_map/all_to_all | solution.py:161
  202.2 4.9 copy-start.14
  205.9 117.4 %collective-permute-start = (bf16[3,2048,256]{2,1,0:T(8,128)(2,1)}, bf16[3,2048,256]{2,1,0:T(8,128)(2,1)}, u32[]{:S(2)}, u32[]{:S(2)}) collective-permute-start(bf16[3,2048,256]{2,1,0:T(8,128)(2,1)} %dynamic-slice_bitcast_fusion), channel_id=1, source_target_pairs={{0,1},{1,0},{2,3},{3,2},{4,5},{5,4},{6,7},{7,6},{8,9},{9,8},{10,11... | collective-permute-start | bytes 9437192 | tf_op jit(solution)/shard_map/ppermute | solution.py:153
  300.1 59.1 %all-to-all-start.5 = ((bf16[32,3,64,256]{3,2,1,0:T(8,128)(2,1)}), bf16[32,3,64,256]{3,2,1,0:T(8,128)(2,1)}, u32[]{:S(2)}, u32[]{:S(2)}) async-start(bf16[32,3,64,256]{3,2,1,0:T(8,128)(2,1)} %broadcast_select_fusion), calls=%async_computation.6 | async-start | bytes 6291456 | tf_op jit(solution)/shard_map/all_to_all | solution.py:192
  317.8 5.5 %copy-start.2 = (bf16[1280,2048]{1,0:T(8,128)(2,1)S(1)}, bf16[1280,2048]{1,0:T(8,128)(2,1)}, u32[]{:S(2)}) copy-start(bf16[1280,2048]{1,0:T(8,128)(2,1)} %reshape.351) | copy-start | bytes 15728644
  359.2 9.8 %copy-start.8 = (f32[64,8]{0,1:T(8,128)S(1)}, f32[64,8]{0,1:T(8,128)}, u32[]{:S(2)}) copy-start(f32[64,8]{0,1:T(8,128)} %param.30) | copy-start | bytes 6148
  359.2 107.7 %all-to-all-start.3 = ((bf16[128,10,2048]{2,1,0:T(8,128)(2,1)}), bf16[128,10,2048]{2,1,0:T(8,128)(2,1)}, u32[]{:S(2)}, u32[]{:S(2)}) async-start(bf16[128,10,2048]{2,1,0:T(8,128)(2,1)} %reshape.352), calls=%async_computation.4 | async-start | bytes 16777216 | tf_op jit(solution)/shard_map/all_to_all | solution.py:174
  495.5 13.0 %copy-start.1 = (bf16[512,2048]{1,0:T(8,128)(2,1)S(1)}, bf16[512,2048]{1,0:T(8,128)(2,1)}, u32[]{:S(2)}) copy-start(bf16[512,2048]{1,0:T(8,128)(2,1)} %param.27) | copy-start | bytes 6291460
  503.6 4.1 copy-start.3
Sparse Core Ops, SparseCore 0:
  72.6 53.3 reduce-scatter.1

commit v3 on v2

--- a/solution.py
+++ b/solution.py
@@ -151,15 +151,24 @@
     give_part = lax.dynamic_index_in_dim(slot_weights, 1 - pair_bit, 0, keepdims=False)
     swap = [(e, e ^ 1) for e in range(exp_count)]
     got_part = lax.ppermute(give_part, "exp", perm=swap)
+    lanes = 128
+    tile_rows = capacity * model_width // lanes
+
+    def as_tiles(rows):
+        return rows.reshape(req_count * exp_count, tile_rows, lanes)
+
+    def as_rows(tiles):
+        return tiles.reshape(req_count * exp_count * capacity, model_width)
+
     send_rows = jnp.repeat(normed, topk_count, axis=0)
     outbox = jnp.zeros((slot_total * capacity, model_width), jnp.bfloat16).at[target].set(send_rows)
-    outbox = outbox.reshape(req_count, 1, slots_here, capacity, model_width)
+    outbox = outbox.reshape(req_count, 1, slots_here * capacity * model_width)
     copies = jnp.broadcast_to(
-        outbox, (req_count, pair_count, slots_here, capacity, model_width)
-    )
-    copies = copies.reshape(req_count * exp_count, capacity, model_width)
+        outbox, (req_count, pair_count, slots_here * capacity * model_width)
+    )
+    copies = as_tiles(copies)
     inbox = lax.all_to_all(copies, ("req", "exp"), split_axis=0, concat_axis=0, tiled=True)
-    in_rows = inbox.reshape(req_count * exp_count * capacity, model_width)
+    in_rows = as_rows(inbox)
     halves = []
     for part in (own_part, got_part):
         gate_act = jnp.dot(in_rows, part[0], preferred_element_type=jnp.float32)
@@ -169,18 +178,17 @@
             hidden, part[2], (((1,), (1,)), ((), ())), preferred_element_type=jnp.float32
         )
         halves.append(piece.astype(jnp.bfloat16).astype(jnp.float32))
-    partial_value = (halves[0] + halves[1]).astype(jnp.bfloat16)
-    partial_value = partial_value.reshape(req_count * exp_count, capacity, model_width)
-    returned = lax.all_to_all(
-        partial_value, ("req", "exp"), split_axis=0, concat_axis=0, tiled=True
-    )
-    result = jnp.sum(
-        returned.astype(jnp.float32).reshape(
-            req_count, pair_count, slots_here * capacity, model_width
-        ),
-        axis=1,
-    )
-    result_rows = jnp.take(result.reshape(slot_total * capacity, model_width), target, axis=0)
+    partial_value = as_tiles((halves[0] + halves[1]).astype(jnp.bfloat16))
+    returned = as_rows(
+        lax.all_to_all(partial_value, ("req", "exp"), split_axis=0, concat_axis=0, tiled=True)
+    )
+    dest_req = row_slot // slots_here
+    dest_pos = row_slot % slots_here
+    result_rows = None
+    for pair_num in range(pair_count):
+        where_from = (dest_req * exp_count + pair_num * slots_here + dest_pos) * capacity + row_rank
+        one = jnp.take(returned, where_from, axis=0).astype(jnp.float32)
+        result_rows = one if result_rows is None else result_rows + one
     mixture = jnp.sum(
         result_rows.reshape(tok_dev, topk_count, model_width) * gate_values[:, :, None], axis=1
     )

time: 524 us -> 429 us (0.82)
  waiting for transfers between devices: 267 us -> 178 us
  other arithmetic: 32.3 us -> 20.3 us
  local copies, waits for them, and re-layouts: 104 us -> 115 us
    all_to_all x1, waiting for transfers between devices: 93.8 us -> 59.8 us  [body(): lax.all_to_all(partial_value, ('req', 'exp'), split_axis=0, concat_axis=0...]
    all_to_all x1, waiting for transfers between devices: 75.4 us -> 41.5 us  [body(): lax.all_to_all(copies, ('req', 'exp'), split_axis=0, concat_axis=0, tiled...]
    all_to_all x1, waiting for transfers between devices: 38.9 us -> 17.9 us  [body(): lax.all_to_all(slot_weights, 'req', split_axis=2, concat_axis=0, tiled=True)]
    reduce_sum x1 -> x0, other arithmetic: 9.42 us -> none  [body(): jnp.sum(returned.astype(jnp.float32).reshape(req_count, pair_count, slots...]
    gather x1 -> x2, local copies, waits for them, and re-layouts: 8.1 us -> 16.9 us  [body(): one = jnp.take(returned, where_from, axis=0).astype(jnp.float32)]
    unnamed x38 -> x36, local copies, waits for them, and re-layouts: 15 us -> 15 us
  transfers between devices with their start and end apart: 8 -> 8, of which waited for: 5 -> 5; matrix products, arithmetic and copies ran while one was open for 24% -> 33% of each run, Pallas kernels for 0% -> 0%
where the time goes in v3:
time: 429 us; the launch traced here: 422 us
  waiting for transfers between devices  178 us (41%)
  local copies, waits for them, and re-layouts  115 us (27%)
  starting transfers between devices  55.2 us (13%)
  matrix products  38.4 us (9%)
  other arithmetic  20.3 us (5%)
  between operations  14.8 us (3%)
    all_to_all x1, waiting for transfers between devices, body(): lax.all_to_all(partial_value, ('req', 'exp'), split_axis=0, concat_axis=0...  59.8 us
    reduce_scatter x1, waiting for transfers between devices, body(): lax.psum_scatter(jnp.dot(attended, out_proj, preferred_element_type=jnp.f...  51.5 us
    all_to_all x1, waiting for transfers between devices, body(): lax.all_to_all(copies, ('req', 'exp'), split_axis=0, concat_axis=0, tiled...  41.5 us
    dot_general x2, matrix products, body(): lax.dot_general(hidden, part[2], (((1,), (1,)), ((), ())), preferred_elem...  23.6 us
    reshape x2, local copies, waits for them, and re-layouts, as_tiles(): return rows.reshape(req_count * exp_count, tile_rows, lanes)  22 us
    all_to_all x1, waiting for transfers between devices, body(): lax.all_to_all(slot_weights, 'req', split_axis=2, concat_axis=0, tiled=True)  17.9 us
    reshape x2, local copies, waits for them, and re-layouts, as_rows(): return tiles.reshape(req_count * exp_count * capacity, model_width)  17.6 us
    all_to_all x1, starting transfers between devices, body(): lax.all_to_all(copies, ('req', 'exp'), split_axis=0, concat_axis=0, tiled...  17.2 us
  transfers between devices with their start and end apart: 8, of which 5 were waited for; matrix products, arithmetic and copies ran while one was open for 33% of the time, Pallas kernels for 0%

profile of v3, /device:TPU:1, one launch (start us, length us, event | category | flops | bytes accessed | tf_op | source)
XLA Modules:
  0.0 422.3 jit_solution(551376000389374354)
XLA Ops:
  9.9 9.8 %all-to-all-start = ((bf16[32,2,1,1024]{3,1,2,0:T(2,128)(2,1)}), bf16[32,2,1,1024]{3,1,2,0:T(2,128)(2,1)S(1)}, u32[]{:S(2)}, u32[]{:S(2)}) async-start(bf16[32,2,1,1024]{3,1,2,0:T(2,128)(2,1)} %maximum_bitcast_fusion), calls=%async_computation | async-start | bytes 262144 | tf_op jit(solution)/shard_map/all_to_all | solution.py:90
  30.5 10.5 %copy.97 = bf16[2,3,2048,256]{3,1,0,2:T(4,128)(2,1)} copy(bf16[2,3,2048,256]{3,2,1,0:T(8,128)(2,1)} %param.35) | data formatting | bytes 12582912 | tf_op args[16]
  42.7 7.7 %all-to-all-start.1 = ((bf16[32,2,1,1024]{3,1,2,0:T(2,128)(2,1)}), bf16[32,2,1,1024]{3,1,2,0:T(2,128)(2,1)S(1)}, u32[]{:S(2)}, u32[]{:S(2)}) async-start(bf16[32,2,1,1024]{3,1,2,0:T(2,128)(2,1)} %broadcast_select_fusion.1), calls=%async_computation.1 | async-start | bytes 262144 | tf_op jit(solution)/shard_map/all_to_all | solution.py:94
  50.6 7.4 %all-to-all-done.1 = bf16[32,2,1,1024]{3,1,2,0:T(2,128)(2,1)S(1)} async-done(((bf16[32,2,1,1024]{3,1,2,0:T(2,128)(2,1)}), bf16[32,2,1,1024]{3,1,2,0:T(2,128)(2,1)S(1)}, u32[]{:S(2)}, u32[]{:S(2)}) %all-to-all-start.1) | async-done | bytes 131104 | tf_op jit(solution)/shard_map/all_to_all | solution.py:94
  72.3 51.5 %reduce-scatter.2.cloned.1.call-done = f32[64,2048]{1,0:T(8,128)} async-done(((f32[256,2048]{1,0:T(8,128)}), f32[64,2048]{1,0:T(8,128)}) %reduce-scatter.2.cloned.1.call-update) | async-done | bytes 524304 | tf_op jit(solution)/shard_map/reduce_scatter | solution.py:121
  126.2 5.4 %scatter_custom_fusion = bf16[640,2048]{1,0:T(8,128)(2,1)} fusion(s32[512]{0:T(512)S(1)} %bitcast.118, bf16[]{:T(256)} %constant.142.clone.1, bf16[64,2048]{1,0:T(8,128)(2,1)S(1)} %multiply_convert_fusion.1), kind=kCustom, calls=%fused_computation.15 | custom fusion | bytes 2883586 | tf_op jit(solution)/shard_map/scatter | solution.py:164
  131.6 6.4 %broadcast_in_dim.196 = bf16[32,40960]{1,0:T(8,128)(2,1)} reshape(bf16[640,2048]{1,0:T(8,128)(2,1)} %scatter_custom_fusion) | data formatting | bytes 5242880 | tf_op jit(solution)/shard_map/broadcast_in_dim | solution.py:166
  138.0 6.9 %broadcast_in_dim.197 = bf16[32,2,40960]{2,1,0:T(2,128)(2,1)} broadcast(bf16[32,40960]{1,0:T(8,128)(2,1)} %broadcast_in_dim.196), dimensions={0,2} | broadcast | bytes 7864320 | tf_op jit(solution)/shard_map/broadcast_in_dim | solution.py:166
  144.9 13.1 %reshape.335 = bf16[128,160,128]{2,1,0:T(8,128)(2,1)} reshape(bf16[32,2,40960]{2,1,0:T(2,128)(2,1)} %broadcast_in_dim.197) | data formatting | bytes 10485760 | tf_op jit(solution)/shard_map/reshape | solution.py:158
  157.9 17.9 %all-to-all-done.4 = bf16[2,3,2048,256]{3,1,0,2:T(4,128)(2,1)} async-done(((bf16[2,3,2048,256]{3,1,0,2:T(4,128)(2,1)}), bf16[2,3,2048,256]{3,1,0,2:T(4,128)(2,1)}, u32[]{:S(2)}, u32[]{:S(2)}) %all-to-all-start.4) | async-done | bytes 6291488 | tf_op jit(solution)/shard_map/all_to_all | solution.py:196
  175.9 17.2 %all-to-all-start.2 = ((bf16[128,160,128]{2,1,0:T(8,128)(2,1)}), bf16[128,160,128]{2,1,0:T(8,128)(2,1)}, u32[]{:S(2)}, u32[]{:S(2)}) async-start(bf16[128,160,128]{2,1,0:T(8,128)(2,1)} %reshape.335), calls=%async_computation.3 | async-start | bytes 10485760 | tf_op jit(solution)/shard_map/all_to_all | solution.py:170
  206.4 5.2 %gather_fusion.1 = bf16[32,3,64,256]{3,2,1,0:T(8,128)(2,1)} fusion(bf16[64,3,64,256]{3,2,1,0:T(8,128)(2,1)} %bitcast.110, s32[1024]{0:T(1024)S(1)} %pad_clamp_fusion), kind=kCustom, calls=%fused_computation.3 | custom fusion | bytes 6291584 | tf_op jit(solution)/shard_map/jit(_take)/gather | solution.py:199
  215.5 41.5 %all-to-all-done.2 = bf16[128,160,128]{2,1,0:T(8,128)(2,1)} async-done(((bf16[128,160,128]{2,1,0:T(8,128)(2,1)}), bf16[128,160,128]{2,1,0:T(8,128)(2,1)}, u32[]{:S(2)}, u32[]{:S(2)}) %all-to-all-start.2) | async-done | bytes 5242912 | tf_op jit(solution)/shard_map/all_to_all | solution.py:170
  257.0 5.0 %all-to-all-start.5 = ((bf16[32,3,64,256]{3,2,1,0:T(8,128)(2,1)}), bf16[32,3,64,256]{3,2,1,0:T(8,128)(2,1)}, u32[]{:S(2)}, u32[]{:S(2)}) async-start(bf16[32,3,64,256]{3,2,1,0:T(8,128)(2,1)} %broadcast_select_fusion), calls=%async_computation.6 | async-start | bytes 6291456 | tf_op jit(solution)/shard_map/all_to_all | solution.py:200
  262.0 8.8 %reshape.336 = bf16[1280,2048]{1,0:T(8,128)(2,1)} reshape(bf16[128,160,128]{2,1,0:T(8,128)(2,1)} %all-to-all-done.2) | data formatting | bytes 10485760 | tf_op jit(solution)/shard_map/reshape | solution.py:161
  270.8 5.5 %fusion.11 = f32[1280,256]{1,0:T(8,128)} fusion(bf16[1280,2048]{1,0:T(8,128)(2,1)} %reshape.336, bf16[2,3,2048,256]{3,2,1,0:T(8,128)(2,1)} %param.35, s32[]{:T(128)S(6)} %select_n.168), kind=kOutput, calls=%fused_computation.33 | convolution fusion | flops 1342177280 | bytes 7602180 | tf_op jit(solution)/shard_map/dot_general | solution.py:174
  279.2 11.2 %convolution_convert_fusion.1 = bf16[1280,2048]{1,0:T(8,128)(2,1)} fusion(bf16[1280,2048]{1,0:T(8,128)(2,1)} %reshape.336, f32[1280,256]{1,0:T(8,128)} %fusion.11, bf16[2,3,2048,256]{3,2,1,0:T(8,128)(2,1)} %param.35, s32[]{:T(128)S(6)} %select_n.168, s32[]{:T(128)S(6)} %add.225, s32[]{:T(128)S(6)} %add.224), kind=kOutput, calls=%fused_computation.8 | convolution fusion | flops 2688942080 | bytes 13895680 | tf_op jit(solution)/shard_map/dot_general | solution.py:177
  290.4 12.5 %add_convert_fusion = bf16[1280,2048]{1,0:T(8,128)(2,1)} fusion(bf16[1280,2048]{1,0:T(8,128)(2,1)} %convolution_convert_fusion.1, bf16[3,2048,256]{2,1,0:T(8,128)(2,1)} %collective-permute-done, f32[1280,256]{1,0:T(8,128)S(1)} %fusion.10, bf16[1280,2048]{1,0:T(8,128)(2,1)} %reshape.336), kind=kOutput, calls=%fused_computation.6 | convolution fusion | flops 2699427840 | bytes 19136512 | tf_op jit(solution)/shard_map/dot_general | solution.py:177
  302.8 8.9 %reshape.337 = bf16[128,160,128]{2,1,0:T(8,128)(2,1)} reshape(bf16[1280,2048]{1,0:T(8,128)(2,1)} %add_convert_fusion) | data formatting | bytes 10485760 | tf_op jit(solution)/shard_map/reshape | solution.py:158
  311.8 8.9 %all-to-all-start.3 = ((bf16[128,160,128]{2,1,0:T(8,128)(2,1)}), bf16[128,160,128]{2,1,0:T(8,128)(2,1)}, u32[]{:S(2)}, u32[]{:S(2)}) async-start(bf16[128,160,128]{2,1,0:T(8,128)(2,1)} %reshape.337), calls=%async_computation.4 | async-start | bytes 10485760 | tf_op jit(solution)/shard_map/all_to_all | solution.py:183
  324.8 59.8 %all-to-all-done.3 = bf16[128,160,128]{2,1,0:T(8,128)(2,1)} async-done(((bf16[128,160,128]{2,1,0:T(8,128)(2,1)}), bf16[128,160,128]{2,1,0:T(8,128)(2,1)}, u32[]{:S(2)}, u32[]{:S(2)}) %all-to-all-start.3) | async-done | bytes 5242912 | tf_op jit(solution)/shard_map/all_to_all | solution.py:183
  384.6 8.8 %reshape.338 = bf16[1280,2048]{1,0:T(8,128)(2,1)} reshape(bf16[128,160,128]{2,1,0:T(8,128)(2,1)} %all-to-all-done.3) | data formatting | bytes 10485760 | tf_op jit(solution)/shard_map/reshape | solution.py:161
  393.4 8.4 %gather_fusion.3 = bf16[512,2048]{1,0:T(8,128)(2,1)} fusion(bf16[1280,2048]{1,0:T(8,128)(2,1)} %reshape.338, s32[1024]{0:T(1024)S(1)} %get-tuple-element.38), kind=kCustom, calls=%fused_computation.1.clone | custom fusion | bytes 4196352 | tf_op jit(solution)/shard_map/jit(_take)/gather | solution.py:190
  401.8 8.5 %gather_fusion.2 = bf16[512,2048]{1,0:T(8,128)(2,1)} fusion(bf16[1280,2048]{1,0:T(8,128)(2,1)} %reshape.338, s32[1024]{0:T(1024)S(1)} %get-tuple-element.39), kind=kCustom, calls=%fused_computation.clone | custom fusion | bytes 4196352 | tf_op jit(solution)/shard_map/jit(_take)/gather | solution.py:190
  (118 shorter events, 60.6 us)
Async XLA Ops:
  7.2 61.0 %copy-start = (bf16[512,2048]{1,0:T(8,128)(2,1)S(1)}, bf16[512,2048]{1,0:T(8,128)(2,1)}, u32[]{:S(2)}) copy-start(bf16[512,2048]{1,0:T(8,128)(2,1)} %param.29) | copy-start | bytes 6291460
  7.2 20.4 %copy-start.10 = (f32[128]{0:T(128)S(1)}, f32[128]{0:T(128)}, u32[]{:S(2)}) copy-start(f32[128]{0:T(128)} %param.24) | copy-start | bytes 1540
  7.2 20.4 %copy-start.11 = (f32[128]{0:T(128)S(1)}, f32[128]{0:T(128)}, u32[]{:S(2)}) copy-start(f32[128]{0:T(128)} %param.23) | copy-start | bytes 1540
  9.9 31.1 %all-to-all-start = ((bf16[32,2,1,1024]{3,1,2,0:T(2,128)(2,1)}), bf16[32,2,1,1024]{3,1,2,0:T(2,128)(2,1)S(1)}, u32[]{:S(2)}, u32[]{:S(2)}) async-start(bf16[32,2,1,1024]{3,1,2,0:T(2,128)(2,1)} %maximum_bitcast_fusion), calls=%async_computation | async-start | bytes 262144 | tf_op jit(solution)/shard_map/all_to_all | solution.py:90
  25.9 4.3 %copy-start.5 = (bf16[256,512]{1,0:T(8,128)(2,1)S(1)}, bf16[256,512]{1,0:T(8,128)(2,1)}, u32[]{:S(2)}) copy-start(bf16[256,512]{1,0:T(8,128)(2,1)} %param.22) | copy-start | bytes 786436
  30.5 10.5 %copy-start.9 = (s32[64]{0:T(128)S(1)}, s32[64]{0:T(128)}, u32[]{:S(2)}) copy-start(s32[64]{0:T(128)} %fusion.43) | copy-start | bytes 772
  42.7 15.3 %all-to-all-start.1 = ((bf16[32,2,1,1024]{3,1,2,0:T(2,128)(2,1)}), bf16[32,2,1,1024]{3,1,2,0:T(2,128)(2,1)S(1)}, u32[]{:S(2)}, u32[]{:S(2)}) async-start(bf16[32,2,1,1024]{3,1,2,0:T(2,128)(2,1)} %broadcast_select_fusion.1), calls=%async_computation.1 | async-start | bytes 262144 | tf_op jit(solution)/shard_map/all_to_all | solution.py:94
  58.0 117.8 %all-to-all-start.4 = ((bf16[2,3,2048,256]{3,1,0,2:T(4,128)(2,1)}), bf16[2,3,2048,256]{3,1,0,2:T(4,128)(2,1)}, u32[]{:S(2)}, u32[]{:S(2)}) async-start(bf16[2,3,2048,256]{3,1,0,2:T(4,128)(2,1)} %copy.97), calls=%async_computation.5 | async-start | bytes 16777216 | tf_op jit(solution)/shard_map/all_to_all | solution.py:196
  63.0 60.8 %reduce-scatter.2.cloned.1.call-start = ((), (), s32[]{:S(2)}) async-start(), calls=%async_computation.7 | async-start | bytes 2621440 | tf_op jit(solution)/shard_map/reduce_scatter | solution.py:121
  68.1 2.1 copy-start.7
  68.2 3.9 copy-start.12
  68.2 55.6 %copy-start.4 = (bf16[64,2048]{1,0:T(8,128)(2,1)S(1)}, bf16[64,2048]{1,0:T(8,128)(2,1)}, u32[]{:S(2)}) copy-start(bf16[64,2048]{1,0:T(8,128)(2,1)} %param.19) | copy-start | bytes 786436
  68.2 56.8 %copy-start.6 = (f32[2048]{0:T(1024)S(1)}, f32[2048]{0:T(1024)}, u32[]{:S(2)}) copy-start(f32[2048]{0:T(1024)} %param.30) | copy-start | bytes 24580
  175.9 81.1 %all-to-all-start.2 = ((bf16[128,160,128]{2,1,0:T(8,128)(2,1)}), bf16[128,160,128]{2,1,0:T(8,128)(2,1)}, u32[]{:S(2)}, u32[]{:S(2)}) async-start(bf16[128,160,128]{2,1,0:T(8,128)(2,1)} %reshape.335), calls=%async_computation.3 | async-start | bytes 10485760 | tf_op jit(solution)/shard_map/all_to_all | solution.py:170
  193.1 4.9 %copy-start.13 = (s32[32]{0:T(128)S(1)}, s32[32]{0:T(128)}, u32[]{:S(2)}) copy-start(s32[32]{0:T(128)} %param.34) | copy-start | bytes 388
  196.9 79.5 %collective-permute-start = (bf16[3,2048,256]{2,1,0:T(8,128)(2,1)}, bf16[3,2048,256]{2,1,0:T(8,128)(2,1)}, u32[]{:S(2)}, u32[]{:S(2)}) collective-permute-start(bf16[3,2048,256]{2,1,0:T(8,128)(2,1)} %dynamic-slice_bitcast_fusion), channel_id=1, source_target_pairs={{0,1},{1,0},{2,3},{3,2},{4,5},{5,4},{6,7},{7,6},{8,9},{9,8},{10,11... | collective-permute-start | bytes 9437192 | tf_op jit(solution)/shard_map/ppermute | solution.py:153
  257.0 54.7 %all-to-all-start.5 = ((bf16[32,3,64,256]{3,2,1,0:T(8,128)(2,1)}), bf16[32,3,64,256]{3,2,1,0:T(8,128)(2,1)}, u32[]{:S(2)}, u32[]{:S(2)}) async-start(bf16[32,3,64,256]{3,2,1,0:T(8,128)(2,1)} %broadcast_select_fusion), calls=%async_computation.6 | async-start | bytes 6291456 | tf_op jit(solution)/shard_map/all_to_all | solution.py:200
  270.8 5.5 %copy-start.2 = (bf16[1280,2048]{1,0:T(8,128)(2,1)S(1)}, bf16[1280,2048]{1,0:T(8,128)(2,1)}, u32[]{:S(2)}) copy-start(bf16[1280,2048]{1,0:T(8,128)(2,1)} %reshape.336) | copy-start | bytes 15728644
  311.8 8.9 %copy-start.8 = (f32[64,8]{0,1:T(8,128)S(1)}, f32[64,8]{0,1:T(8,128)}, u32[]{:S(2)}) copy-start(f32[64,8]{0,1:T(8,128)} %param.32) | copy-start | bytes 6148
  311.8 72.8 %all-to-all-start.3 = ((bf16[128,160,128]{2,1,0:T(8,128)(2,1)}), bf16[128,160,128]{2,1,0:T(8,128)(2,1)}, u32[]{:S(2)}, u32[]{:S(2)}) async-start(bf16[128,160,128]{2,1,0:T(8,128)(2,1)} %reshape.337), calls=%async_computation.4 | async-start | bytes 10485760 | tf_op jit(solution)/shard_map/all_to_all | solution.py:183
  410.3 4.1 copy-start.3
  410.3 4.9 %copy-start.1 = (bf16[512,2048]{1,0:T(8,128)(2,1)S(1)}, bf16[512,2048]{1,0:T(8,128)(2,1)}, u32[]{:S(2)}) copy-start(bf16[512,2048]{1,0:T(8,128)(2,1)} %param.29) | copy-start | bytes 6291460
Sparse Core Ops, SparseCore 0:
  70.4 53.3 reduce-scatter.1

commit v4 on v3

--- a/solution.py
+++ b/solution.py
@@ -1,9 +1,125 @@
+import functools
 import math
 
 import jax
 import jax.numpy as jnp
 from jax import lax
+from jax.experimental import pallas as pl
+from jax.experimental.pallas import tpu as pltpu
 from jax.sharding import PartitionSpec as P
+
+MESH = pl.DeviceIdType.MESH
+
+
+def cache_kernel(n, need_ref, both_ref, out_ref, stage, send_buf, land, sems):
+    me = lax.axis_index("req")
+    ex = lax.axis_index("exp")
+    barrier = pltpu.get_barrier_semaphore()
+
+    def greet(k, carry):
+        peer = lax.rem(me + k, n)
+        pl.semaphore_signal(barrier, inc=1, device_id=(peer, ex), device_id_type=MESH)
+        return carry
+
+    lax.fori_loop(1, n, greet, 0)
+    pl.semaphore_wait(barrier, n - 1)
+
+    def first_copy(k, peer):
+        return pltpu.make_async_remote_copy(
+            src_ref=both_ref.at[peer],
+            dst_ref=stage.at[me],
+            send_sem=sems.at[0, k],
+            recv_sem=sems.at[1, k],
+            device_id=(peer, ex),
+            device_id_type=MESH,
+        )
+
+    def second_copy(k, peer):
+        return pltpu.make_async_remote_copy(
+            src_ref=send_buf.at[k],
+            dst_ref=land.at[me],
+            send_sem=sems.at[2, k],
+            recv_sem=sems.at[3, k],
+            device_id=(peer, ex),
+            device_id_type=MESH,
+        )
+
+    def send_first(k, carry):
+        first_copy(k, lax.rem(me + k, n)).start()
+        return carry
+
+    lax.fori_loop(1, n, send_first, 0)
+    stage[me] = both_ref[me]
+
+    def wait_first(k, carry):
+        source = lax.rem(me + n - k, n)
+        pltpu.make_async_remote_copy(
+            src_ref=both_ref.at[me],
+            dst_ref=stage.at[source],
+            send_sem=sems.at[0, k],
+            recv_sem=sems.at[1, k],
+            device_id=(source, ex),
+            device_id_type=MESH,
+        ).wait_recv()
+        return carry
+
+    lax.fori_loop(1, n, wait_first, 0)
+    rows = lax.broadcasted_iota(jnp.int32, both_ref.shape[1:], 0)
+
+    def pieces_for(dest):
+        picked = []
+        for c in range(2):
+            block = need_ref[dest * 2 + c]
+            slab = stage[block // 2].astype(jnp.float32)
+            one = jnp.where(block % 2 == 0, slab[0:1], slab[1:2])
+            picked.append(jnp.broadcast_to(one, slab.shape))
+        return jnp.where(rows == 0, picked[0], picked[1]).astype(land.dtype)
+
+    def send_second(k, carry):
+        dest = lax.rem(me + k, n)
+        send_buf[k] = pieces_for(dest)
+        second_copy(k, dest).start()
+        return carry
+
+    lax.fori_loop(1, n, send_second, 0)
+    land[me] = pieces_for(me)
+
+    def wait_second(k, carry):
+        source = lax.rem(me + n - k, n)
+        pltpu.make_async_remote_copy(
+            src_ref=send_buf.at[k],
+            dst_ref=land.at[source],
+            send_sem=sems.at[2, k],
+            recv_sem=sems.at[3, k],
+            device_id=(source, ex),
+            device_id_type=MESH,
+        ).wait_recv()
+        first_copy(k, lax.rem(me + k, n)).wait_send()
+        second_copy(k, lax.rem(me + k, n)).wait_send()
+        return carry
+
+    lax.fori_loop(1, n, wait_second, 0)
+    out_ref[...] = land[...]
+
+
+def exchange_cache(both_t, need_flat, n):
+    shape = both_t.shape
+    return pl.pallas_call(
+        functools.partial(cache_kernel, n),
+        out_shape=jax.ShapeDtypeStruct(shape, both_t.dtype),
+        in_specs=[
+            pl.BlockSpec(memory_space=pltpu.SMEM),
+            pl.BlockSpec(memory_space=pltpu.VMEM),
+        ],
+        out_specs=pl.BlockSpec(memory_space=pltpu.VMEM),
+        scratch_shapes=[
+            pltpu.VMEM(shape, both_t.dtype),
+            pltpu.VMEM(shape, both_t.dtype),
+            pltpu.VMEM(shape, both_t.dtype),
+            pltpu.SemaphoreType.DMA((4, n)),
+        ],
+        compiler_params=pltpu.CompilerParams(collective_id=0, has_side_effects=True),
+    )(need_flat, both_t)
 
 
 def prepare(values, gain, position):
@@ -84,15 +200,10 @@
     need_blocks, need_requests = compact(block_rows, cache_dev)
     my_requests = lax.dynamic_index_in_dim(need_requests, group_idx, 0, keepdims=False)
     key_width = cache_keys.shape[2]
-    rows_per = pre_len // req_count
     both = jnp.concatenate([cache_keys, cache_values], axis=-1)
-    both = both.reshape(cache_dev, req_count, rows_per, 2 * key_width).transpose(1, 0, 2, 3)
-    spread = lax.all_to_all(both, "req", split_axis=0, concat_axis=0, tiled=True)
-    spread = spread.reshape(req_count * cache_dev, rows_per, 2 * key_width)
-    picked = jnp.take(spread, need_blocks.reshape(-1), axis=0)
-    picked = picked.reshape(req_count, cache_dev, rows_per, 2 * key_width)
-    gathered = lax.all_to_all(picked, "req", split_axis=0, concat_axis=0, tiled=True)
-    gathered = gathered.transpose(1, 0, 2, 3).reshape(cache_dev, pre_len, 2 * key_width)
+    both_t = both.transpose(1, 0, 2)
+    gathered = exchange_cache(both_t, need_blocks.reshape(-1).astype(jnp.int32), req_count)
+    gathered = gathered.transpose(1, 0, 2)
     far_keys = gathered[..., :key_width]
     far_values = gathered[..., key_width:]
     query_n = prepare(query_in.reshape(tok_grp, head_count, head_size), query_gain, position)

time: 429 us -> 512 us (1.19)
  Pallas kernels: 0 us -> 146 us
  waiting for transfers between devices: 178 us -> 140 us
  starting transfers between devices: 55.2 us -> 33.3 us
    pallas_call x0 -> x1, Pallas kernels: none -> 146 us  [exchange_cache(): pl.pallas_call(functools.partial(cache_kernel, n), out_shape=jax.ShapeDty...]
    all_to_all x1, waiting for transfers between devices: 17.9 us -> 0.01 us  [body(): lax.all_to_all(slot_weights, 'req', split_axis=2, concat_axis=0, tiled=True)]
    all_to_all x2 -> x0, starting transfers between devices: 17.5 us -> none  [the longest x1 9.81 us: body(): lax.all_to_all(both, 'req', split_axis=0, concat_axis=0, tiled=True)]
    reduce_scatter x1, waiting for transfers between devices: 51.5 us -> 38.2 us  [body(): lax.psum_scatter(jnp.dot(attended, out_proj, preferred_element_type=jnp.f...]
    all_to_all x1, starting transfers between devices: 17.2 us -> 8.12 us  [body(): lax.all_to_all(copies, ('req', 'exp'), split_axis=0, concat_axis=0, tiled...]
    all_to_all x2 -> x0, waiting for transfers between devices: 7.45 us -> none  [the longest x1 7.45 us: body(): lax.all_to_all(picked, 'req', split_axis=0, concat_axis=0, tiled=True)]
    all_to_all x1, starting transfers between devices: 4.96 us -> 10.1 us  [body(): lax.all_to_all(slot_weights, 'req', split_axis=2, concat_axis=0, tiled=True)]
    unnamed x36 -> x46, local copies, waits for them, and re-layouts: 15 us -> 11.4 us
  transfers between devices with their start and end apart: 8 -> 6, of which waited for: 5 -> 3; matrix products, arithmetic and copies ran while one was open for 33% -> 25% of each run, Pallas kernels for 0% -> 29%
where the time goes in v4:
time: 512 us; the launch traced here: 502 us
  Pallas kernels  146 us (29%)
  waiting for transfers between devices  140 us (27%)
  local copies, waits for them, and re-layouts  113 us (22%)
  matrix products  38.9 us (8%)
  starting transfers between devices  33.3 us (7%)
  other arithmetic  16.9 us (3%)
  between operations  14.8 us (3%)
    pallas_call x1, Pallas kernels, exchange_cache(): pl.pallas_call(functools.partial(cache_kernel, n), out_shape=jax.ShapeDty...  146 us
    all_to_all x1, waiting for transfers between devices, body(): lax.all_to_all(partial_value, ('req', 'exp'), split_axis=0, concat_axis=0...  59.8 us
    all_to_all x1, waiting for transfers between devices, body(): lax.all_to_all(copies, ('req', 'exp'), split_axis=0, concat_axis=0, tiled...  41.5 us
    reduce_scatter x1, waiting for transfers between devices, body(): lax.psum_scatter(jnp.dot(attended, out_proj, preferred_element_type=jnp.f...  38.2 us
    dot_general x2, matrix products, body(): lax.dot_general(hidden, part[2], (((1,), (1,)), ((), ())), preferred_elem...  23.6 us
    reshape x2, local copies, waits for them, and re-layouts, as_tiles(): return rows.reshape(req_count * exp_count, tile_rows, lanes)  22 us
    reshape x2, local copies, waits for them, and re-layouts, as_rows(): return tiles.reshape(req_count * exp_count * capacity, model_width)  17.6 us
    gather x2, local copies, waits for them, and re-layouts, body(): one = jnp.take(returned, where_from, axis=0).astype(jnp.float32)  16.9 us
  transfers between devices with their start and end apart: 6, of which 3 were waited for; matrix products, arithmetic and copies ran while one was open for 25% of the time, Pallas kernels for 29%

profile of v4, /device:TPU:1, one launch (start us, length us, event | category | flops | bytes accessed | tf_op | source)
XLA Modules:
  0.0 502.2 jit_solution(17801678095203038198)
XLA Ops:
  7.2 10.6 %copy.97 = bf16[2,3,2048,256]{3,1,0,2:T(4,128)(2,1)} copy(bf16[2,3,2048,256]{3,2,1,0:T(8,128)(2,1)} %param.35) | data formatting | bytes 12582912 | tf_op args[16]
  17.9 10.1 %all-to-all-start.2 = ((bf16[2,3,2048,256]{3,1,0,2:T(4,128)(2,1)}), bf16[2,3,2048,256]{3,1,0,2:T(4,128)(2,1)}, u32[]{:S(2)}, u32[]{:S(2)}) async-start(bf16[2,3,2048,256]{3,1,0,2:T(4,128)(2,1)} %copy.97), calls=%async_computation.3 | async-start | bytes 16777216 | tf_op jit(solution)/shard_map/all_to_all | solution.py:307
  30.7 146.1 %shard_map.176 = bf16[32,2,1024]{2,1,0:T(2,128)(2,1)} custom-call(s32[64]{0:T(128)} %reshape.260.need_ref, bf16[32,2,1024]{2,1,0:T(2,128)(2,1)} %maximum_bitcast_fusion.both_ref), custom_call_target="tpu_custom_call" | custom-call | tf_op jit(solution)/shard_map/pallas_call | solution.py:107
  192.1 38.2 %reduce-scatter.2.cloned.1.call-done = f32[64,2048]{1,0:T(8,128)} async-done(((f32[256,2048]{1,0:T(8,128)}), f32[64,2048]{1,0:T(8,128)}) %reduce-scatter.2.cloned.1.call-update) | async-done | bytes 524304 | tf_op jit(solution)/shard_map/reduce_scatter | solution.py:232
  232.7 5.8 %scatter_custom_fusion = bf16[640,2048]{1,0:T(8,128)(2,1)} fusion(s32[512]{0:T(512)S(1)} %bitcast.108, bf16[]{:T(256)} %constant.127.clone.1, bf16[64,2048]{1,0:T(8,128)(2,1)S(1)} %multiply_convert_fusion.1), kind=kCustom, calls=%fused_computation.14 | custom fusion | bytes 2883586 | tf_op jit(solution)/shard_map/scatter | solution.py:275
  238.5 6.4 %broadcast_in_dim.184 = bf16[32,40960]{1,0:T(8,128)(2,1)} reshape(bf16[640,2048]{1,0:T(8,128)(2,1)} %scatter_custom_fusion) | data formatting | bytes 5242880 | tf_op jit(solution)/shard_map/broadcast_in_dim | solution.py:277
  244.9 6.9 %broadcast_in_dim.185 = bf16[32,2,40960]{2,1,0:T(2,128)(2,1)} broadcast(bf16[32,40960]{1,0:T(8,128)(2,1)} %broadcast_in_dim.184), dimensions={0,2} | broadcast | bytes 7864320 | tf_op jit(solution)/shard_map/broadcast_in_dim | solution.py:277
  251.9 13.1 %reshape.269 = bf16[128,160,128]{2,1,0:T(8,128)(2,1)} reshape(bf16[32,2,40960]{2,1,0:T(2,128)(2,1)} %broadcast_in_dim.185) | data formatting | bytes 10485760 | tf_op jit(solution)/shard_map/reshape | solution.py:269
  264.9 8.1 %all-to-all-start = ((bf16[128,160,128]{2,1,0:T(8,128)(2,1)}), bf16[128,160,128]{2,1,0:T(8,128)(2,1)}, u32[]{:S(2)}, u32[]{:S(2)}) async-start(bf16[128,160,128]{2,1,0:T(8,128)(2,1)} %reshape.269), calls=%async_computation.1 | async-start | bytes 10485760 | tf_op jit(solution)/shard_map/all_to_all | solution.py:281
  278.2 4.9 copy.98
  286.4 5.2 %gather_fusion = bf16[32,3,64,256]{3,2,1,0:T(8,128)(2,1)} fusion(bf16[64,3,64,256]{3,2,1,0:T(8,128)(2,1)} %bitcast.100, s32[1024]{0:T(1024)S(1)} %pad_clamp_fusion), kind=kCustom, calls=%fused_computation.2 | custom fusion | bytes 6291584 | tf_op jit(solution)/shard_map/jit(_take)/gather | solution.py:310
  295.5 41.5 %all-to-all-done = bf16[128,160,128]{2,1,0:T(8,128)(2,1)} async-done(((bf16[128,160,128]{2,1,0:T(8,128)(2,1)}), bf16[128,160,128]{2,1,0:T(8,128)(2,1)}, u32[]{:S(2)}, u32[]{:S(2)}) %all-to-all-start) | async-done | bytes 5242912 | tf_op jit(solution)/shard_map/all_to_all | solution.py:281
  337.0 5.0 all-to-all-start.3
  342.0 8.8 %reshape.270 = bf16[1280,2048]{1,0:T(8,128)(2,1)} reshape(bf16[128,160,128]{2,1,0:T(8,128)(2,1)} %all-to-all-done) | data formatting | bytes 10485760 | tf_op jit(solution)/shard_map/reshape | solution.py:272
  350.8 5.5 %fusion.11 = f32[1280,256]{1,0:T(8,128)} fusion(bf16[1280,2048]{1,0:T(8,128)(2,1)} %reshape.270, bf16[2,3,2048,256]{3,2,1,0:T(8,128)(2,1)} %param.35, s32[]{:T(128)S(6)} %select_n.135), kind=kOutput, calls=%fused_computation.32 | convolution fusion | flops 1342177280 | bytes 7602180 | tf_op jit(solution)/shard_map/dot_general | solution.py:285
  359.2 11.2 %convolution_convert_fusion.1 = bf16[1280,2048]{1,0:T(8,128)(2,1)} fusion(bf16[1280,2048]{1,0:T(8,128)(2,1)} %reshape.270, f32[1280,256]{1,0:T(8,128)} %fusion.11, bf16[2,3,2048,256]{3,2,1,0:T(8,128)(2,1)} %param.35, s32[]{:T(128)S(6)} %select_n.135, s32[]{:T(128)S(6)} %add.199, s32[]{:T(128)S(6)} %add.198), kind=kOutput, calls=%fused_computation.7 | convolution fusion | flops 2688942080 | bytes 13895680 | tf_op jit(solution)/shard_map/dot_general | solution.py:288
  370.3 12.5 %add_convert_fusion = bf16[1280,2048]{1,0:T(8,128)(2,1)} fusion(bf16[1280,2048]{1,0:T(8,128)(2,1)} %convolution_convert_fusion.1, bf16[3,2048,256]{2,1,0:T(8,128)(2,1)} %collective-permute-done, f32[1280,256]{1,0:T(8,128)S(1)} %fusion.10, bf16[1280,2048]{1,0:T(8,128)(2,1)} %reshape.270), kind=kOutput, calls=%fused_computation.5 | convolution fusion | flops 2699427840 | bytes 19136512 | tf_op jit(solution)/shard_map/dot_general | solution.py:288
  382.8 8.9 %reshape.271 = bf16[128,160,128]{2,1,0:T(8,128)(2,1)} reshape(bf16[1280,2048]{1,0:T(8,128)(2,1)} %add_convert_fusion) | data formatting | bytes 10485760 | tf_op jit(solution)/shard_map/reshape | solution.py:269
  391.7 8.9 %all-to-all-start.1 = ((bf16[128,160,128]{2,1,0:T(8,128)(2,1)}), bf16[128,160,128]{2,1,0:T(8,128)(2,1)}, u32[]{:S(2)}, u32[]{:S(2)}) async-start(bf16[128,160,128]{2,1,0:T(8,128)(2,1)} %reshape.271), calls=%async_computation.2 | async-start | bytes 10485760 | tf_op jit(solution)/shard_map/all_to_all | solution.py:294
  404.7 59.8 %all-to-all-done.1 = bf16[128,160,128]{2,1,0:T(8,128)(2,1)} async-done(((bf16[128,160,128]{2,1,0:T(8,128)(2,1)}), bf16[128,160,128]{2,1,0:T(8,128)(2,1)}, u32[]{:S(2)}, u32[]{:S(2)}) %all-to-all-start.1) | async-done | bytes 5242912 | tf_op jit(solution)/shard_map/all_to_all | solution.py:294
  464.6 8.8 %reshape.272 = bf16[1280,2048]{1,0:T(8,128)(2,1)} reshape(bf16[128,160,128]{2,1,0:T(8,128)(2,1)} %all-to-all-done.1) | data formatting | bytes 10485760 | tf_op jit(solution)/shard_map/reshape | solution.py:272
  473.4 8.4 %gather_fusion.2 = bf16[512,2048]{1,0:T(8,128)(2,1)} fusion(bf16[1280,2048]{1,0:T(8,128)(2,1)} %reshape.272, s32[1024]{0:T(1024)S(1)} %get-tuple-element.38), kind=kCustom, calls=%fused_computation.1.clone | custom fusion | bytes 4196352 | tf_op jit(solution)/shard_map/jit(_take)/gather | solution.py:301
  481.8 8.5 %gather_fusion.1 = bf16[512,2048]{1,0:T(8,128)(2,1)} fusion(bf16[1280,2048]{1,0:T(8,128)(2,1)} %reshape.272, s32[1024]{0:T(1024)S(1)} %get-tuple-element.39), kind=kCustom, calls=%fused_computation.clone | custom fusion | bytes 4196352 | tf_op jit(solution)/shard_map/jit(_take)/gather | solution.py:301
  490.3 4.0 fusion.1
  (117 shorter events, 40.0 us)
Async XLA Ops:
  7.2 180.8 %copy-start = (bf16[512,2048]{1,0:T(8,128)(2,1)S(1)}, bf16[512,2048]{1,0:T(8,128)(2,1)}, u32[]{:S(2)}) copy-start(bf16[512,2048]{1,0:T(8,128)(2,1)} %param.29) | copy-start | bytes 6291460
  17.8 10.2 %copy-start.16 = (s32[1,4]{1,0:T(1,128)S(1)}, s32[1,4]{1,0:T(1,128)}, u32[]{:S(2)}) copy-start(s32[1,4]{1,0:T(1,128)} %param.28) | copy-start | bytes 52
  17.8 10.4 %copy-start.13 = (s32[128]{0:T(128)S(1)}, s32[128]{0:T(128)}, u32[]{:S(2)}) copy-start(s32[128]{0:T(128)} %param.27) | copy-start | bytes 1540
  17.8 12.0 %copy-start.8 = (bf16[2,32,512]{2,1,0:T(8,128)(2,1)S(1)}, bf16[2,32,512]{2,1,0:T(8,128)(2,1)}, u32[]{:S(2)}) copy-start(bf16[2,32,512]{2,1,0:T(8,128)(2,1)} %param.25) | copy-start | bytes 196612
  17.8 12.0 %copy-start.9 = (bf16[2,32,512]{2,1,0:T(8,128)(2,1)S(1)}, bf16[2,32,512]{2,1,0:T(8,128)(2,1)}, u32[]{:S(2)}) copy-start(bf16[2,32,512]{2,1,0:T(8,128)(2,1)} %param.26) | copy-start | bytes 196612
  17.8 160.8 %copy-start.5 = (bf16[256,512]{1,0:T(8,128)(2,1)S(1)}, bf16[256,512]{1,0:T(8,128)(2,1)}, u32[]{:S(2)}) copy-start(bf16[256,512]{1,0:T(8,128)(2,1)} %param.20) | copy-start | bytes 786436
  17.8 161.0 %copy-start.6 = (bf16[256,512]{1,0:T(8,128)(2,1)S(1)}, bf16[256,512]{1,0:T(8,128)(2,1)}, u32[]{:S(2)}) copy-start(bf16[256,512]{1,0:T(8,128)(2,1)} %param.21) | copy-start | bytes 786436
  17.9 247.1 %all-to-all-start.2 = ((bf16[2,3,2048,256]{3,1,0,2:T(4,128)(2,1)}), bf16[2,3,2048,256]{3,1,0,2:T(4,128)(2,1)}, u32[]{:S(2)}, u32[]{:S(2)}) async-start(bf16[2,3,2048,256]{3,1,0,2:T(4,128)(2,1)} %copy.97), calls=%async_computation.3 | async-start | bytes 16777216 | tf_op jit(solution)/shard_map/all_to_all | solution.py:307
  27.9 151.1 %copy-start.7 = (bf16[256,512]{1,0:T(8,128)(2,1)S(1)}, bf16[256,512]{1,0:T(8,128)(2,1)}, u32[]{:S(2)}) copy-start(bf16[256,512]{1,0:T(8,128)(2,1)} %param.22) | copy-start | bytes 786436
  28.0 202.3 %reduce-scatter.2.cloned.1.call-start = ((), (), s32[]{:S(2)}) async-start(), calls=%async_computation.5 | async-start | bytes 2621440 | tf_op jit(solution)/shard_map/reduce_scatter | solution.py:232
  29.8 151.3 %copy-start.14 = (f32[128]{0:T(128)S(1)}, f32[128]{0:T(128)}, u32[]{:S(2)}) copy-start(f32[128]{0:T(128)} %param.24) | copy-start | bytes 1540
  29.8 151.3 %copy-start.15 = (f32[128]{0:T(128)S(1)}, f32[128]{0:T(128)}, u32[]{:S(2)}) copy-start(f32[128]{0:T(128)} %param.23) | copy-start | bytes 1540
  188.0 3.9 copy-start.17
  188.0 42.3 %copy-start.4 = (bf16[64,2048]{1,0:T(8,128)(2,1)S(1)}, bf16[64,2048]{1,0:T(8,128)(2,1)}, u32[]{:S(2)}) copy-start(bf16[64,2048]{1,0:T(8,128)(2,1)} %param.19) | copy-start | bytes 786436
  188.0 43.5 %copy-start.10 = (f32[2048]{0:T(1024)S(1)}, f32[2048]{0:T(1024)}, u32[]{:S(2)}) copy-start(f32[2048]{0:T(1024)} %param.30) | copy-start | bytes 24580
  264.9 72.1 %all-to-all-start = ((bf16[128,160,128]{2,1,0:T(8,128)(2,1)}), bf16[128,160,128]{2,1,0:T(8,128)(2,1)}, u32[]{:S(2)}, u32[]{:S(2)}) async-start(bf16[128,160,128]{2,1,0:T(8,128)(2,1)} %reshape.269), calls=%async_computation.1 | async-start | bytes 10485760 | tf_op jit(solution)/shard_map/all_to_all | solution.py:281
  273.1 4.9 copy-start.18
  276.8 79.5 %collective-permute-start = (bf16[3,2048,256]{2,1,0:T(8,128)(2,1)}, bf16[3,2048,256]{2,1,0:T(8,128)(2,1)}, u32[]{:S(2)}, u32[]{:S(2)}) collective-permute-start(bf16[3,2048,256]{2,1,0:T(8,128)(2,1)} %dynamic-slice_bitcast_fusion), channel_id=1, source_target_pairs={{0,1},{1,0},{2,3},{3,2},{4,5},{5,4},{6,7},{7,6},{8,9},{9,8},{10,11... | collective-permute-start | bytes 9437192 | tf_op jit(solution)/shard_map/ppermute | solution.py:264
  337.0 54.7 %all-to-all-start.3 = ((bf16[32,3,64,256]{3,2,1,0:T(8,128)(2,1)}), bf16[32,3,64,256]{3,2,1,0:T(8,128)(2,1)}, u32[]{:S(2)}, u32[]{:S(2)}) async-start(bf16[32,3,64,256]{3,2,1,0:T(8,128)(2,1)} %broadcast_select_fusion), calls=%async_computation.4 | async-start | bytes 6291456 | tf_op jit(solution)/shard_map/all_to_all | solution.py:311
  350.8 5.6 %copy-start.2 = (bf16[1280,2048]{1,0:T(8,128)(2,1)S(1)}, bf16[1280,2048]{1,0:T(8,128)(2,1)}, u32[]{:S(2)}) copy-start(bf16[1280,2048]{1,0:T(8,128)(2,1)} %reshape.270) | copy-start | bytes 15728644
  391.7 8.9 %copy-start.12 = (f32[64,8]{0,1:T(8,128)S(1)}, f32[64,8]{0,1:T(8,128)}, u32[]{:S(2)}) copy-start(f32[64,8]{0,1:T(8,128)} %param.32) | copy-start | bytes 6148
  391.7 72.8 %all-to-all-start.1 = ((bf16[128,160,128]{2,1,0:T(8,128)(2,1)}), bf16[128,160,128]{2,1,0:T(8,128)(2,1)}, u32[]{:S(2)}, u32[]{:S(2)}) async-start(bf16[128,160,128]{2,1,0:T(8,128)(2,1)} %reshape.271), calls=%async_computation.2 | async-start | bytes 10485760 | tf_op jit(solution)/shard_map/all_to_all | solution.py:294
  490.3 4.1 copy-start.3
  490.3 4.9 copy-start.1
  (1 other events, 2.1 us)
Sparse Core Ops, SparseCore 0:
  190.2 40.0 reduce-scatter.1
